TPU v7x, 256 devices: a whole 4x4x8 slice. The times are simulated.
256 devices in a mesh: ctx: 64 (over z, y, core), head: 4 (over x).
Axes of the slice: x: 4, y: 4, z: 8, core: 2. Of those that a mesh axis runs over, the one named last changes fastest.
Arguments:
- queries: bfloat16 [65536, 1024], P('ctx', 'head'), may hold values from -6 to 6
- key_rows: bfloat16 [65536, 128], P('ctx'), may hold values from -6 to 6
- value_rows: bfloat16 [65536, 128], P('ctx'), may hold values from -6 to 6
- out_grad: bfloat16 [65536, 1024], P('ctx', 'head'), may hold values from -6 to 6
- block_lists: int32 [512, 8], P('ctx'), may hold values from -1 to 511, as said below
Outputs:
- attended: bfloat16 [65536, 1024], P('ctx', 'head')
- query_grad: bfloat16 [65536, 1024], P('ctx', 'head')
- key_grad: bfloat16 [65536, 128], P(('ctx', 'head'))
- value_grad: bfloat16 [65536, 128], P(('ctx', 'head'))
Inputs may be any that keep to these rules, and one draw needn't show every extreme that they name: `block_lists`: entry 0 of row b is the position block of row b's own tokens. Every other entry is -1 or a block lying wholly before it whose rows belong to another index of ctx; the blocks of one row are distinct. Over the 8 rows of one index of ctx, at most 1 entries name blocks of any one other index, and in every draw some index has exactly 1 entries on one other.
All inputs are finite; a program needn't handle non-finite values.
Results may differ from a plain program's by a relative error of at most 0.022.
Values may be sent and summed in bfloat16 or wider, within the bound.
A program may use at most 128 MiB of HBM per device.

v0:
```python
import math

import jax
import jax.numpy as jnp
from jax import lax
from jax.sharding import PartitionSpec as P

HD = 128
BLK = 128
SEL = 8
QB = 8


NEG_FILL = -1e30


def block_home(block, half_blocks, pair_count):
    stretch_idx = block // half_blocks
    early_side = stretch_idx < pair_count
    owner_dev = jnp.where(early_side, stretch_idx, 2 * pair_count - 1 - stretch_idx)
    local_blk = block % half_blocks + jnp.where(early_side, 0, half_blocks)
    return (owner_dev, local_blk)


def entry_slots(list_rows, half_blocks, pair_count):
    extras = list_rows[:, 1:].reshape(-1)
    usable = extras >= 0
    owner_dev, local_blk = block_home(jnp.maximum(extras, 0), half_blocks, pair_count)
    onehot_own = (
        (owner_dev[:, None] == jnp.arange(pair_count, dtype=jnp.int32)[None, :]) & usable[:, None]
    ).astype(jnp.int32)
    running = jnp.cumsum(onehot_own, axis=0)
    rank_in = jnp.sum(onehot_own * running, axis=1) - 1
    return (owner_dev, local_blk, rank_in, usable)


def on_device(queries, key_rows, value_rows, out_grad, block_lists):
    pair_count = lax.axis_size("ctx")
    half_blocks = QB // 2
    capacity = (QB * (SEL - 1) + pair_count - 2) // (pair_count - 1)
    total_slots = pair_count * capacity
    device = lax.axis_index("ctx")
    score_scale = 1.0 / math.sqrt(HD)
    owner_dev, local_blk, rank_in, usable = entry_slots(block_lists, half_blocks, pair_count)
    slot_idx = jnp.where(usable, owner_dev * capacity + rank_in, total_slots)
    req_table = (
        jnp.full((total_slots + 1,), -1, jnp.int32).at[slot_idx].set(local_blk)[:total_slots]
    )
    requested = lax.all_to_all(
        req_table.reshape(pair_count, capacity), "ctx", split_axis=0, concat_axis=0, tiled=True
    )
    kv_blocks = jnp.stack([key_rows.reshape(QB, BLK, HD), value_rows.reshape(QB, BLK, HD)], axis=1)
    send_blocks = kv_blocks[jnp.maximum(requested, 0)]
    fetched = lax.all_to_all(send_blocks, "ctx", split_axis=0, concat_axis=0, tiled=True)
    kv_table = jnp.concatenate([kv_blocks, fetched.reshape(total_slots, 2, BLK, HD)], axis=0)
    local_ids = jnp.arange(QB, dtype=jnp.int32)
    remote_idx = jnp.where(usable, QB + slot_idx, 0).reshape(QB, SEL - 1)
    entry_idx = jnp.concatenate([local_ids[:, None], remote_idx], axis=1)
    kv_tiles = kv_table[entry_idx]
    key_tile = kv_tiles[:, :, 0]
    value_tile = kv_tiles[:, :, 1]
    own_block = jnp.where(
        local_ids < half_blocks,
        device * half_blocks + local_ids,
        (2 * pair_count - 1 - device) * half_blocks + local_ids - half_blocks,
    )
    offsets = jnp.arange(BLK, dtype=jnp.int32)
    query_pos = own_block[:, None] * BLK + offsets[None, :]
    key_pos = jnp.maximum(block_lists, 0)[:, :, None] * BLK + offsets[None, None, :]
    visible = (block_lists >= 0)[:, None, :, None] & (
        key_pos[:, None, :, :] <= query_pos[:, :, None, None]
    )
    heads_here = queries.shape[1] // HD
    q_blocks = queries.reshape(QB, BLK, heads_here, HD)
    g_blocks = out_grad.reshape(QB, BLK, heads_here, HD)
    scores = (
        jnp.einsum("qihd,qsjd->qhisj", q_blocks, key_tile, preferred_element_type=jnp.float32)
        * score_scale
    )
    scores = jnp.where(visible[:, None], scores, NEG_FILL)
    row_max = jnp.max(scores, axis=(3, 4), keepdims=True)
    weights = jnp.exp(scores - row_max)
    row_total = jnp.sum(weights, axis=(3, 4), keepdims=True)
    summed = jnp.einsum(
        "qhisj,qsjd->qihd",
        weights.astype(jnp.bfloat16),
        value_tile,
        preferred_element_type=jnp.float32,
    )
    attended = (summed / jnp.transpose(row_total[..., 0, 0], (0, 2, 1))[..., None]).astype(
        jnp.bfloat16
    )
    log_total = row_max + jnp.log(row_total)
    probability = jnp.exp(scores - log_total)
    row_delta = jnp.sum(g_blocks.astype(jnp.float32) * attended.astype(jnp.float32), axis=3)
    grad_p = jnp.einsum(
        "qihd,qsjd->qhisj", g_blocks, value_tile, preferred_element_type=jnp.float32
    )
    grad_s = (probability * (grad_p - jnp.transpose(row_delta, (0, 2, 1))[..., None, None])).astype(
        jnp.bfloat16
    )
    query_grad = (
        jnp.einsum("qhisj,qsjd->qihd", grad_s, key_tile, preferred_element_type=jnp.float32)
        * score_scale
    ).astype(jnp.bfloat16)
    key_part = (
        jnp.einsum("qhisj,qihd->qsjd", grad_s, q_blocks, preferred_element_type=jnp.float32)
        * score_scale
    )
    value_part = jnp.einsum(
        "qhisj,qihd->qsjd",
        probability.astype(jnp.bfloat16),
        g_blocks,
        preferred_element_type=jnp.float32,
    )
    grad_tiles = jnp.stack([key_part, value_part], axis=2)
    outgoing = (
        jnp.zeros((total_slots + 1, 2, BLK, HD), jnp.float32)
        .at[slot_idx]
        .add(grad_tiles[:, 1:].reshape(QB * (SEL - 1), 2, BLK, HD))[:total_slots]
    )
    outgoing = outgoing.reshape(pair_count, capacity, 2, BLK, HD)
    returned = lax.all_to_all(
        outgoing.astype(jnp.bfloat16), "ctx", split_axis=0, concat_axis=0, tiled=True
    ).astype(outgoing.dtype)
    target = jnp.where(requested >= 0, requested, QB)
    own_total = jnp.concatenate([grad_tiles[:, 0], jnp.zeros((1, 2, BLK, HD), jnp.float32)], axis=0)
    own_total = own_total.at[target].add(returned)[:QB]
    combined = jnp.transpose(own_total, (1, 0, 2, 3)).reshape(2, QB * BLK, HD)
    reduced = lax.psum_scatter(
        combined.astype(jnp.bfloat16), "head", scatter_dimension=1, tiled=True
    ).astype(jnp.float32)
    return (
        attended.reshape(QB * BLK, heads_here * HD),
        query_grad.reshape(QB * BLK, heads_here * HD),
        reduced[0].astype(jnp.bfloat16),
        reduced[1].astype(jnp.bfloat16),
    )


def solution(mesh):
    return jax.shard_map(
        on_device,
        mesh=mesh,
        in_specs=(
            P("ctx", "head"),
            P("ctx", None),
            P("ctx", None),
            P("ctx", "head"),
            P("ctx", None),
        ),
        out_specs=(
            P("ctx", "head"),
            P("ctx", "head"),
            P(("ctx", "head"), None),
            P(("ctx", "head"), None),
        ),
        check_vma=False,
    )
```

profile of v0, /device:TPU:8, one launch (start us, length us, event | category | flops | bytes accessed | tf_op | source)
XLA Modules:
  0.0 355.6 jit_solution(3629999580469385326)
XLA Ops:
  7.2 0.8 sign_compare_fusion
  7.9 0.1 ge.31
  8.0 0.1 ge.30
  8.1 0.8 fusion.47
  8.9 0.1 div.23
  9.0 0.1 div.22
  9.0 0.1 ne.52
  9.1 0.1 rem.18
  9.2 0.1 fusion.41
  9.3 0.1 reduce_window_sum.11
  9.4 0.2 select_reduce_fusion
  9.6 0.1 sub.84
  9.7 0.8 fusion.46
  10.5 0.1 and.61
  10.6 0.7 scatter_custom_fusion
  11.3 0.7 copy.75
  12.0 12.1 %all-to-all-start = ((s32[64,1,1]{2,1,0:T(1,128)}), s32[64,1,1]{2,1,0:T(1,128)S(1)}, u32[]{:S(2)}, u32[]{:S(2)}) async-start(s32[64,1,1]{2,1,0:T(1,128)} %copy.75), calls=%async_computation | async-start | bytes 65536 | tf_op jit(solution)/shard_map/all_to_all | solution.py:49
  24.1 1.1 pad_maximum_fusion.2
  25.2 7.5 %all-to-all-done = s32[64,1,1]{2,1,0:T(1,128)S(1)} async-done(((s32[64,1,1]{2,1,0:T(1,128)}), s32[64,1,1]{2,1,0:T(1,128)S(1)}, u32[]{:S(2)}, u32[]{:S(2)}) %all-to-all-start) | async-done | bytes 288 | tf_op jit(solution)/shard_map/all_to_all | solution.py:49
  32.7 2.4 fusion.39
  35.1 3.0 gather_fusion
  38.1 0.0 copy-start.4
  38.1 6.6 %all-to-all-start.1 = ((bf16[64,1,2,128,128]{4,3,2,1,0:T(8,128)(2,1)}), bf16[64,1,2,128,128]{4,3,2,1,0:T(8,128)(2,1)}, u32[]{:S(2)}, u32[]{:S(2)}) async-start(bf16[64,1,2,128,128]{4,3,2,1,0:T(8,128)(2,1)} %bitcast.160), calls=%async_computation.1 | async-start | bytes 8388608 | tf_op jit(solution)/shard_map/all_to_all | solution.py:54
  44.8 0.1 compare_select_fusion.2
  44.8 0.1 reshape.292
  44.9 0.1 reshape.336
  45.1 0.4 copy.84
  45.5 0.1 reshape.277
  45.7 0.1 iota_add_fusion.1
  45.8 0.1 iota_add_fusion
  45.8 1.5 compare_and_fusion
  47.3 93.6 %all-to-all-done.1 = bf16[64,1,2,128,128]{4,3,2,1,0:T(8,128)(2,1)} async-done(((bf16[64,1,2,128,128]{4,3,2,1,0:T(8,128)(2,1)}), bf16[64,1,2,128,128]{4,3,2,1,0:T(8,128)(2,1)}, u32[]{:S(2)}, u32[]{:S(2)}) %all-to-all-start.1) | async-done | bytes 4194336 | tf_op jit(solution)/shard_map/all_to_all | solution.py:54
  140.9 4.0 %pad_maximum_fusion.1 = bf16[72,2,128,128]{3,2,1,0:T(8,128)(2,1)} fusion(bf16[64,2,128,128]{3,2,1,0:T(8,128)(2,1)} %bitcast.7, bf16[8,1,128,128]{3,2,1,0:T(8,128)(2,1)S(1)} %bitcast.173, bf16[8,1,128,128]{3,2,1,0:T(8,128)(2,1)S(1)} %bitcast.175), kind=kLoop, calls=%fused_computation.16 | loop fusion | flops 4718592 | bytes 9437184 | tf_op jit(solution)/shard_map/concatenate | solution.py:55
  144.9 5.4 %gather_fusion.1 = bf16[64,2,128,128]{3,2,1,0:T(8,128)(2,1)} fusion(bf16[72,2,128,128]{3,2,1,0:T(8,128)(2,1)} %pad_maximum_fusion.1, s32[1024]{0:T(1024)S(1)} %pad_clamp_fusion), kind=kCustom, calls=%fused_computation.1 | custom fusion | bytes 8388864 | tf_op jit(solution)/shard_map/gather | solution.py:59
  150.4 2.5 copy.77
  152.9 1.5 fusion.5
  154.4 2.2 fusion.2
  156.6 2.6 multiply_reduce_fusion
  159.2 2.1 fusion.20
  161.3 4.2 %fusion.1 = bf16[8,2,128,8,128]{2,4,1,3,0:T(8,128)(2,1)} fusion(f32[8,8,128,128,2]{3,2,4,1,0:T(8,128)S(1)} %get-tuple-element.33, f32[8,2,128]{2,1,0:T(2,128)S(1)} %bitcast.181, f32[8,2,128]{2,1,0:T(2,128)S(1)} %bitcast.180, pred[8,128,8,128]{1,3,2,0:T(8,128)(4,1)S(1)} %compare_and_fusion, bf16[8,8,2,128,128]{4,3,1,0,2:T(8,128)(2,1)S(1)} %bitcast.163, ...), kind=kOutput, calls=%fused_computation.8 | convolution fusion | flops 549453824 | bytes 16269312 | tf_op jit(solution)/shard_map/qihd,qsjd->qhisj/dot_general | solution.py:96
  165.5 3.4 fusion.11
  169.0 0.9 pad_maximum_fusion
  169.9 1.3 copy-done
  171.2 4.0 %copy.90 = f32[56,2,128,128]{3,2,1,0:T(8,128)} copy(f32[56,2,128,128]{3,2,0,1:T(8,128)S(1)} %bitcast.159) | data formatting | bytes 14680064 | tf_op jit(solution)/shard_map/reshape | solution.py:120
  175.1 4.3 %broadcast_in_dim.23 = f32[65,2,128,128]{3,2,1,0:T(8,128)} broadcast(f32[]{:T(128)} %constant.87.clone.1), dimensions={} | broadcast | bytes 8519684 | tf_op jit(solution)/shard_map/broadcast_in_dim | solution.py:118
  179.5 18.9 %scatter_fusion = f32[65,2,128,128]{3,2,1,0:T(8,128)} fusion(f32[65,2,128,128]{3,2,1,0:T(8,128)} %broadcast_in_dim.23, s32[56]{0:T(128)S(1)} %fusion.53, f32[56,2,128,128]{3,2,1,0:T(8,128)} %copy.90), kind=kCustom, calls=%fused_computation.3 | custom fusion | flops 1835008 | bytes 22020320 | tf_op jit(solution)/shard_map/scatter-add | solution.py:120
  198.4 6.3 %fusion.10 = bf16[64,1,2,128,128]{4,3,2,1,0:T(8,128)(2,1)} fusion(f32[65,2,128,128]{3,2,1,0:T(8,128)} %scatter_fusion), kind=kLoop, calls=%fused_computation.20 | loop fusion | bytes 8388608 | tf_op jit(solution)/shard_map/convert_element_type | solution.py:124
  204.7 5.9 %all-to-all-start.2 = ((bf16[64,1,2,128,128]{4,3,2,1,0:T(8,128)(2,1)}), bf16[64,1,2,128,128]{4,3,2,1,0:T(8,128)(2,1)}, u32[]{:S(2)}, u32[]{:S(2)}) async-start(bf16[64,1,2,128,128]{4,3,2,1,0:T(8,128)(2,1)} %fusion.10), calls=%async_computation.2 | async-start | bytes 8388608 | tf_op jit(solution)/shard_map/all_to_all | solution.py:123
  210.7 0.0 reduce-scatter.2.cloned.1.call-start
  210.7 1.3 maximum_bitcast_fusion
  212.0 0.1 copy.132
  212.1 0.1 concatenate.33.clone
  212.2 94.6 %all-to-all-done.2 = bf16[64,1,2,128,128]{4,3,2,1,0:T(8,128)(2,1)} async-done(((bf16[64,1,2,128,128]{4,3,2,1,0:T(8,128)(2,1)}), bf16[64,1,2,128,128]{4,3,2,1,0:T(8,128)(2,1)}, u32[]{:S(2)}, u32[]{:S(2)}) %all-to-all-start.2) | async-done | bytes 4194336 | tf_op jit(solution)/shard_map/all_to_all | solution.py:123
  306.9 6.5 %bitcast_convert_fusion = f32[64,2,128,128]{3,2,1,0:T(8,128)} fusion(bf16[64,1,2,128,128]{4,3,2,1,0:T(8,128)(2,1)} %all-to-all-done.2), kind=kLoop, calls=%fused_computation.21 | loop fusion | flops 2097152 | bytes 12582912 | tf_op jit(solution)/shard_map/convert_element_type | solution.py:125
  313.3 12.3 %scatter_fusion.1 = f32[9,2,128,128]{3,2,1,0:T(8,128)S(1)} fusion(f32[9,2,128,128]{3,2,1,0:T(8,128)S(1)} %concatenate.33.clone, s32[64]{0:T(128)S(1)} %get-tuple-element.20, f32[64,2,128,128]{3,2,1,0:T(8,128)} %bitcast_convert_fusion), kind=kCustom, calls=%fused_computation.4 | custom fusion | flops 2097152 | bytes 25166080 | tf_op jit(solution)/shard_map/scatter-add | solution.py:128
  325.7 0.1 fusion.34
  325.8 0.9 copy.93
  326.7 0.0 reduce-scatter.2.cloned.1.call-update
  326.7 0.4 copy.115
  327.1 3.7 %fusion.31 = bf16[8,128,2,128]{1,3,2,0:T(8,128)(2,1)S(1)} fusion(bf16[8,2,128,8,128]{2,4,1,3,0:T(8,128)(2,1)} %fusion.1, bf16[8,8,2,128,128]{4,3,1,0,2:T(8,128)(2,1)} %bitcast.164), kind=kOutput, calls=%fused_computation.42 | convolution fusion | flops 537395200 | bytes 6815744 | tf_op jit(solution)/shard_map/qhisj,qsjd->qihd/dot_general | solution.py:103
  330.8 0.4 copy.124
  331.3 1.1 copy_bitcast_fusion
  332.4 14.8 %reduce-scatter.2.cloned.1.call-done = bf16[2,256,128]{2,1,0:T(8,128)(2,1)} async-done(((bf16[2,1024,128]{2,1,0:T(8,128)(2,1)}), bf16[2,256,128]{2,1,0:T(8,128)(2,1)}) %reduce-scatter.2.cloned.1.call-update) | async-done | bytes 131088 | tf_op jit(solution)/shard_map/reduce_scatter | solution.py:130
  347.2 1.5 slice_bitcast_fusion.18
  (26 shorter events, 0.1 us)
Async XLA Ops:
  12.0 20.7 %all-to-all-start = ((s32[64,1,1]{2,1,0:T(1,128)}), s32[64,1,1]{2,1,0:T(1,128)S(1)}, u32[]{:S(2)}, u32[]{:S(2)}) async-start(s32[64,1,1]{2,1,0:T(1,128)} %copy.75), calls=%async_computation | async-start | bytes 65536 | tf_op jit(solution)/shard_map/all_to_all | solution.py:49
  38.1 6.8 %copy-start.5 = (bf16[1024,256]{1,0:T(8,128)(2,1)S(1)}, bf16[1024,256]{1,0:T(8,128)(2,1)}, u32[]{:S(2)}) copy-start(bf16[1024,256]{1,0:T(8,128)(2,1)} %param.8) | copy-start | bytes 1572868
  38.1 7.4 %copy-start.6 = (bf16[1024,256]{1,0:T(8,128)(2,1)S(1)}, bf16[1024,256]{1,0:T(8,128)(2,1)}, u32[]{:S(2)}) copy-start(bf16[1024,256]{1,0:T(8,128)(2,1)} %param.5) | copy-start | bytes 1572868
  38.1 7.7 %copy-start.7 = (s32[8,8]{1,0:T(8,128)S(1)}, s32[8,8]{1,0:T(8,128)}, u32[]{:S(2)}) copy-start(s32[8,8]{1,0:T(8,128)} %param.9) | copy-start | bytes 772
  38.1 102.9 %copy-start.3 = (bf16[1024,128]{1,0:T(8,128)(2,1)S(1)}, bf16[1024,128]{1,0:T(8,128)(2,1)}, u32[]{:S(2)}) copy-start(bf16[1024,128]{1,0:T(8,128)(2,1)} %param.7) | copy-start | bytes 786436
  38.1 102.8 %copy-start.4 = (bf16[1024,128]{1,0:T(8,128)(2,1)S(1)}, bf16[1024,128]{1,0:T(8,128)(2,1)}, u32[]{:S(2)}) copy-start(bf16[1024,128]{1,0:T(8,128)(2,1)} %param.6) | copy-start | bytes 786436
  38.1 102.8 %all-to-all-start.1 = ((bf16[64,1,2,128,128]{4,3,2,1,0:T(8,128)(2,1)}), bf16[64,1,2,128,128]{4,3,2,1,0:T(8,128)(2,1)}, u32[]{:S(2)}, u32[]{:S(2)}) async-start(bf16[64,1,2,128,128]{4,3,2,1,0:T(8,128)(2,1)} %bitcast.160), calls=%async_computation.1 | async-start | bytes 8388608 | tf_op jit(solution)/shard_map/all_to_all | solution.py:54
  152.9 8.5 %copy-start.2 = (bf16[64,2,128,128]{3,2,0,1:T(8,128)(2,1)}, bf16[64,2,128,128]{3,2,0,1:T(8,128)(2,1)S(1)}, u32[]{:S(2)}) copy-start(bf16[64,2,128,128]{3,2,0,1:T(8,128)(2,1)S(1)} %copy.77) | copy-start | bytes 12582916
  161.3 7.6 %copy-start.1 = (f32[8,8,1,128,128]{4,3,1,0,2:T(8,128)}, f32[8,8,1,128,128]{4,3,1,0,2:T(8,128)S(1)}, u32[]{:S(2)}) copy-start(f32[8,8,1,128,128]{4,3,1,0,2:T(8,128)S(1)} %fusion.20) | copy-start | bytes 12582916
  169.0 2.2 copy-start
  204.7 102.1 %all-to-all-start.2 = ((bf16[64,1,2,128,128]{4,3,2,1,0:T(8,128)(2,1)}), bf16[64,1,2,128,128]{4,3,2,1,0:T(8,128)(2,1)}, u32[]{:S(2)}, u32[]{:S(2)}) async-start(bf16[64,1,2,128,128]{4,3,2,1,0:T(8,128)(2,1)} %fusion.10), calls=%async_computation.2 | async-start | bytes 8388608 | tf_op jit(solution)/shard_map/all_to_all | solution.py:123
  210.7 136.6 %reduce-scatter.2.cloned.1.call-start = ((), (), s32[]{:S(2)}) async-start(), calls=%async_computation.4 | async-start | bytes 655360 | tf_op jit(solution)/shard_map/reduce_scatter | solution.py:130
Sparse Core Ops, SparseCore 0:
  326.8 20.3 reduce-scatter.1
where the time goes:
time: 356 us
  waiting for transfers between devices  211 us (59%)
  other arithmetic  54 us (15%)
  local copies, waits for them, and re-layouts  34.4 us (10%)
  starting transfers between devices  24.7 us (7%)
  matrix products  17.6 us (5%)
  between operations  14.3 us (4%)
    all_to_all x1, waiting for transfers between devices, on_device(): lax.all_to_all(outgoing.astype(jnp.bfloat16), 'ctx', split_axis=0, concat...  94.6 us
    all_to_all x1, waiting for transfers between devices, on_device(): lax.all_to_all(send_blocks, 'ctx', split_axis=0, concat_axis=0, tiled=True)  93.6 us
    scatter-add x1, other arithmetic, on_device(): outgoing = jnp.zeros((total_slots + 1, 2, BLK, HD), jnp.float32).at[slot_...  18.9 us
    reduce_scatter x1, waiting for transfers between devices, on_device(): lax.psum_scatter(combined.astype(jnp.bfloat16), 'head', scatter_dimension...  14.8 us
    scatter-add x1, other arithmetic, on_device(): own_total = own_total.at[target].add(returned)[:QB]  12.3 us
    all_to_all x1, starting transfers between devices, on_device(): lax.all_to_all(req_table.reshape(pair_count, capacity), 'ctx', split_axis...  12.1 us
    gather x2, local copies, waits for them, and re-layouts, on_device(): kv_tiles = kv_table[entry_idx]  7.93 us
    all_to_all x1, waiting for transfers between devices, on_device(): lax.all_to_all(req_table.reshape(pair_count, capacity), 'ctx', split_axis...  7.46 us
  transfers between devices with their start and end apart: 4, of which 4 were waited for; matrix products, arithmetic and copies ran while one was open for 3% of the time, Pallas kernels for 0%

commit v1 on v0

--- a/solution.py
+++ b/solution.py
@@ -49,9 +49,15 @@
     requested = lax.all_to_all(
         req_table.reshape(pair_count, capacity), "ctx", split_axis=0, concat_axis=0, tiled=True
     )
+    head_count = lax.axis_size("head")
+    head_idx = lax.axis_index("head")
+    part_rows = 2 * BLK // head_count
     kv_blocks = jnp.stack([key_rows.reshape(QB, BLK, HD), value_rows.reshape(QB, BLK, HD)], axis=1)
-    send_blocks = kv_blocks[jnp.maximum(requested, 0)]
-    fetched = lax.all_to_all(send_blocks, "ctx", split_axis=0, concat_axis=0, tiled=True)
+    kv_parts = kv_blocks.reshape(QB, head_count, part_rows, HD)
+    my_part = lax.dynamic_index_in_dim(kv_parts, head_idx, axis=1, keepdims=False)
+    send_parts = my_part[jnp.maximum(requested, 0)]
+    fetched_part = lax.all_to_all(send_parts, "ctx", split_axis=0, concat_axis=0, tiled=True)
+    fetched = lax.all_gather(fetched_part, "head", axis=2, tiled=False)
     kv_table = jnp.concatenate([kv_blocks, fetched.reshape(total_slots, 2, BLK, HD)], axis=0)
     local_ids = jnp.arange(QB, dtype=jnp.int32)
     remote_idx = jnp.where(usable, QB + slot_idx, 0).reshape(QB, SEL - 1)
@@ -114,19 +120,38 @@
         preferred_element_type=jnp.float32,
     )
     grad_tiles = jnp.stack([key_part, value_part], axis=2)
-    outgoing = (
-        jnp.zeros((total_slots + 1, 2, BLK, HD), jnp.float32)
+    entry_count = QB * (SEL - 1)
+    slot_entry = (
+        jnp.full((total_slots + 1,), entry_count, jnp.int32)
         .at[slot_idx]
-        .add(grad_tiles[:, 1:].reshape(QB * (SEL - 1), 2, BLK, HD))[:total_slots]
+        .set(jnp.arange(entry_count, dtype=jnp.int32))[:total_slots]
     )
-    outgoing = outgoing.reshape(pair_count, capacity, 2, BLK, HD)
+    remote_tiles = jnp.concatenate(
+        [grad_tiles[:, 1:].reshape(entry_count, 2, BLK, HD), jnp.zeros((1, 2, BLK, HD), jnp.float32)],
+        axis=0,
+    )
+    remote_parts = jnp.moveaxis(remote_tiles.reshape(entry_count + 1, head_count, part_rows, HD), 1, 0)
+    outgoing = remote_parts[:, slot_entry].astype(jnp.bfloat16)
+    outgoing_part = lax.psum_scatter(
+        outgoing.reshape(head_count * total_slots * part_rows, HD), "head", scatter_dimension=0, tiled=True
+    )
     returned = lax.all_to_all(
-        outgoing.astype(jnp.bfloat16), "ctx", split_axis=0, concat_axis=0, tiled=True
-    ).astype(outgoing.dtype)
-    target = jnp.where(requested >= 0, requested, QB)
-    own_total = jnp.concatenate([grad_tiles[:, 0], jnp.zeros((1, 2, BLK, HD), jnp.float32)], axis=0)
-    own_total = own_total.at[target].add(returned)[:QB]
-    combined = jnp.transpose(own_total, (1, 0, 2, 3)).reshape(2, QB * BLK, HD)
+        outgoing_part.reshape(pair_count, capacity, part_rows, HD),
+        "ctx",
+        split_axis=0,
+        concat_axis=0,
+        tiled=True,
+    ).astype(jnp.float32)
+    target = jnp.where(requested >= 0, requested, QB).reshape(-1)
+    returned_sum = (
+        jnp.zeros((QB + 1, part_rows, HD), jnp.float32)
+        .at[target]
+        .add(returned.reshape(-1, part_rows, HD))[:QB]
+    )
+    own_parts = grad_tiles[:, 0].reshape(QB, head_count, part_rows, HD)
+    mine = (jnp.arange(head_count, dtype=jnp.int32) == head_idx)[None, :, None, None]
+    own_parts = own_parts + jnp.where(mine, returned_sum[:, None], 0.0)
+    combined = jnp.transpose(own_parts.reshape(QB, 2, BLK, HD), (1, 0, 2, 3)).reshape(2, QB * BLK, HD)
     reduced = lax.psum_scatter(
         combined.astype(jnp.bfloat16), "head", scatter_dimension=1, tiled=True
     ).astype(jnp.float32)

time: 356 us -> 286 us (0.80)
  waiting for transfers between devices: 211 us -> 143 us
  blocking collectives: 0 us -> 34.4 us
  other arithmetic: 54 us -> 21.1 us
    all_to_all x2 -> x1, waiting for transfers between devices: 188 us -> 28.5 us  [on_device(): lax.all_to_all(outgoing_part.reshape(pair_count, capacity, part_rows, HD)...]
    reduce_scatter x0 -> x1, waiting for transfers between devices: none -> 49.9 us  [on_device(): lax.psum_scatter(outgoing.reshape(head_count * total_slots * part_rows, H...]
    all_gather x0 -> x1, waiting for transfers between devices: none -> 43.8 us  [on_device(): fetched = lax.all_gather(fetched_part, 'head', axis=2, tiled=False)]
    all_to_all x0 -> x1, blocking collectives: none -> 34.4 us  [on_device(): lax.all_to_all(send_parts, 'ctx', split_axis=0, concat_axis=0, tiled=True)]
    scatter-add x2 -> x1, other arithmetic: 31.2 us -> 3.75 us  [on_device(): returned_sum = jnp.zeros((QB + 1, part_rows, HD), jnp.float32).at[target]...]
    convert_element_type x1, other arithmetic: 6.47 us -> 2.25 us  [on_device(): combined.astype(jnp.bfloat16)]
    broadcast_in_dim x1 -> x4, local copies, waits for them, and re-layouts: 4.35 us -> 0.3 us  [the longest x3 0.27 us: on_device(): own_parts = own_parts + jnp.where(mine, returned_sum[:, None], 0.0)]
    all_to_all x2 -> x1, starting transfers between devices: 12.6 us -> 10.6 us  [on_device(): lax.all_to_all(outgoing_part.reshape(pair_count, capacity, part_rows, HD)...]
  transfers between devices with their start and end apart: 4 -> 5, of which waited for: 4 -> 5; matrix products, arithmetic and copies ran while one was open for 3% -> 4% of each run, Pallas kernels for 0% -> 0%
where the time goes in v1:
time: 286 us
  waiting for transfers between devices  143 us (50%)
  blocking collectives  34.4 us (12%)
  local copies, waits for them, and re-layouts  31.7 us (11%)
  starting transfers between devices  22.8 us (8%)
  other arithmetic  21.1 us (7%)
  matrix products  18.4 us (6%)
  between operations  14.2 us (5%)
    reduce_scatter x1, waiting for transfers between devices, on_device(): lax.psum_scatter(outgoing.reshape(head_count * total_slots * part_rows, H...  49.9 us
    all_gather x1, waiting for transfers between devices, on_device(): fetched = lax.all_gather(fetched_part, 'head', axis=2, tiled=False)  43.8 us
    all_to_all x1, blocking collectives, on_device(): lax.all_to_all(send_parts, 'ctx', split_axis=0, concat_axis=0, tiled=True)  34.4 us
    all_to_all x1, waiting for transfers between devices, on_device(): lax.all_to_all(outgoing_part.reshape(pair_count, capacity, part_rows, HD)...  28.5 us
    reduce_scatter x1, waiting for transfers between devices, on_device(): lax.psum_scatter(combined.astype(jnp.bfloat16), 'head', scatter_dimension...  13.5 us
    all_to_all x1, starting transfers between devices, on_device(): lax.all_to_all(req_table.reshape(pair_count, capacity), 'ctx', split_axis...  12.1 us
    all_to_all x1, starting transfers between devices, on_device(): lax.all_to_all(outgoing_part.reshape(pair_count, capacity, part_rows, HD)...  10.6 us
    gather x2, local copies, waits for them, and re-layouts, on_device(): kv_tiles = kv_table[entry_idx]  7.93 us
  transfers between devices with their start and end apart: 5, of which 5 were waited for; matrix products, arithmetic and copies ran while one was open for 4% of the time, Pallas kernels for 0%

profile of v1, /device:TPU:8, one launch (start us, length us, event | category | flops | bytes accessed | tf_op | source)
XLA Modules:
  0.0 285.7 jit_solution(4333570657018169348)
XLA Ops:
  7.2 0.9 sign_compare_fusion
  8.0 0.8 fusion.46
  8.8 0.1 ge.37
  8.9 0.1 ge.38
  9.0 0.1 div.23
  9.0 0.1 div.22
  9.1 0.1 rem.18
  9.2 0.1 ne.52
  9.3 0.1 fusion.40
  9.4 0.1 reduce_window_sum.11
  9.5 0.2 select_reduce_fusion
  9.7 0.1 sub.84
  9.8 0.8 fusion.45
  10.6 0.1 and.62
  10.7 0.7 scatter_custom_fusion
  11.4 0.7 copy.76
  12.1 12.1 %all-to-all-start = ((s32[64,1,1]{2,1,0:T(1,128)}), s32[64,1,1]{2,1,0:T(1,128)S(1)}, u32[]{:S(2)}, u32[]{:S(2)}) async-start(s32[64,1,1]{2,1,0:T(1,128)} %copy.76), calls=%async_computation | async-start | bytes 65536 | tf_op jit(solution)/shard_map/all_to_all | solution.py:49
  24.3 1.1 pad_maximum_fusion.2
  25.4 7.4 %all-to-all-done = s32[64,1,1]{2,1,0:T(1,128)S(1)} async-done(((s32[64,1,1]{2,1,0:T(1,128)}), s32[64,1,1]{2,1,0:T(1,128)S(1)}, u32[]{:S(2)}, u32[]{:S(2)}) %all-to-all-start) | async-done | bytes 288 | tf_op jit(solution)/shard_map/all_to_all | solution.py:49
  32.8 2.4 fusion.62
  35.2 0.7 gather_fusion
  36.0 34.4 %all_to_all.22 = bf16[64,1,64,128]{3,2,1,0:T(8,128)(2,1)} all-to-all(bf16[64,1,64,128]{3,2,1,0:T(8,128)(2,1)S(1)} %bitcast.185), channel_id=1, replica_groups=mesh['ctx'=64,'head'=4] {'ctx'}, dimensions={0} | all-to-all | bytes 2097152 | tf_op jit(solution)/shard_map/all_to_all | solution.py:59
  70.5 0.1 reshape.335
  70.6 0.1 compare_select_fusion
  70.7 0.1 reshape.356
  70.8 0.1 reshape.411
  70.9 0.4 copy.84
  71.4 0.9 scatter_custom_fusion.1
  72.3 0.1 iota_add_fusion.1
  72.4 0.1 iota_add_fusion
  72.5 1.5 compare_and_fusion
  74.0 43.8 %all-gather.3.cloned.1.call-done = bf16[64,4,64,128]{3,2,1,0:T(8,128)(2,1)} async-done(((bf16[64,1,64,128]{3,2,1,0:T(8,128)(2,1)}), bf16[64,4,64,128]{3,2,1,0:T(8,128)(2,1)}) %all-gather.3.cloned.1.call-update) | async-done | bytes 4194320 | tf_op jit(solution)/shard_map/all_gather | solution.py:60
  117.8 4.0 %pad_maximum_fusion.1 = bf16[72,2,128,128]{3,2,1,0:T(8,128)(2,1)} fusion(bf16[64,2,128,128]{3,2,1,0:T(8,128)(2,1)} %bitcast.190, bf16[8,1,128,128]{3,2,1,0:T(8,128)(2,1)S(1)} %bitcast.200, bf16[8,1,128,128]{3,2,1,0:T(8,128)(2,1)S(1)} %bitcast.202), kind=kLoop, calls=%fused_computation.17 | loop fusion | flops 4718592 | bytes 9437184 | tf_op jit(solution)/shard_map/concatenate | solution.py:61
  121.7 5.4 %gather_fusion.1 = bf16[64,2,128,128]{3,2,1,0:T(8,128)(2,1)} fusion(bf16[72,2,128,128]{3,2,1,0:T(8,128)(2,1)} %pad_maximum_fusion.1, s32[1024]{0:T(1024)S(1)} %pad_clamp_fusion.1), kind=kCustom, calls=%fused_computation.1 | custom fusion | bytes 8388864 | tf_op jit(solution)/shard_map/gather | solution.py:65
  127.2 2.5 copy.77
  129.7 1.5 fusion.5
  131.2 2.2 fusion.2
  133.5 3.3 %multiply_reduce_fusion = (f32[8,128,2]{1,2,0:T(2,128)S(1)}, bf16[8,128,2,128]{1,3,2,0:T(8,128)(2,1)}) fusion(bf16[8,128,2,128]{1,3,2,0:T(8,128)(2,1)S(1)} %copy.84, f32[8,128,2]{1,2,0:T(2,128)S(1)} %bitcast.205, f32[8,8,128,128,2]{3,2,4,1,0:T(8,128)S(1)} %get-tuple-element.33, f32[8,2,128]{2,1,0:T(2,128)S(1)} %get-tuple-element.32, ...), kind=kOutput, calls=%fused_computation.48 | convolution fusion | flops 546830336 | bytes 12607488 | tf_op jit(solution)/shard_map/qhisj,qsjd->qihd/dot_general | solution.py:90
  136.7 2.2 fusion.19
  138.9 4.2 %fusion.1 = bf16[8,2,128,8,128]{2,4,1,3,0:T(8,128)(2,1)} fusion(f32[8,8,128,128,2]{3,2,4,1,0:T(8,128)S(1)} %get-tuple-element.33, f32[8,2,128]{2,1,0:T(2,128)S(1)} %bitcast.209, f32[8,2,128]{2,1,0:T(2,128)S(1)} %bitcast.208, pred[8,128,8,128]{1,3,2,0:T(8,128)(4,1)S(1)} %compare_and_fusion, bf16[8,8,2,128,128]{4,3,1,0,2:T(8,128)(2,1)S(1)} %bitcast.188, ...), kind=kOutput, calls=%fused_computation.8 | convolution fusion | flops 549453824 | bytes 16269312 | tf_op jit(solution)/shard_map/qihd,qsjd->qhisj/dot_general | solution.py:102
  143.1 3.4 %fusion.10 = f32[8,8,1,128,128]{4,3,1,0,2:T(8,128)S(1)} fusion(bf16[8,2,128,8,128]{2,4,1,3,0:T(8,128)(2,1)} %fusion.1, bf16[8,128,2,128,1]{3,2,1,0,4:T(2,128)(2,1)S(1)} %bitcast.192), kind=kOutput, calls=%fused_computation.22 | convolution fusion | flops 537919488 | bytes 8912896 | tf_op jit(solution)/shard_map/qhisj,qihd->qsjd/dot_general | solution.py:113
  146.6 0.7 pad_maximum_fusion
  147.3 1.2 copy-done
  148.5 0.4 copy.90
  149.0 0.5 concatenate.33
  149.5 2.7 copy.151
  152.1 5.1 %gather_fusion.2 = bf16[64,4,64,128]{3,2,1,0:T(8,128)(2,1)} fusion(bf16[4,57,64,128]{3,2,1,0:T(8,128)(2,1)} %bitcast.179, s32[1024]{0:T(1024)S(1)} %pad_clamp_fusion), kind=kCustom, calls=%fused_computation.2 | custom fusion | bytes 8388864 | tf_op jit(solution)/shard_map/gather | solution.py:134
  157.2 5.5 %copy.92 = bf16[4,64,64,128]{3,2,1,0:T(8,128)(2,1)} copy(bf16[4,64,64,128]{3,2,0,1:T(8,128)(2,1)} %bitcast.181) | data formatting | bytes 8388608 | tf_op jit(solution)/shard_map/convert_element_type | solution.py:134
  162.7 49.9 %reduce-scatter.3.cloned.1.call-done = bf16[4096,128]{1,0:T(8,128)(2,1)} async-done(((bf16[16384,128]{1,0:T(8,128)(2,1)}), bf16[4096,128]{1,0:T(8,128)(2,1)}) %reduce-scatter.3.cloned.1.call-update) | async-done | bytes 1048592 | tf_op jit(solution)/shard_map/reduce_scatter | solution.py:135
  212.6 10.6 %all-to-all-start.2 = ((bf16[64,1,64,128]{3,2,1,0:T(8,128)(2,1)}), bf16[64,1,64,128]{3,2,1,0:T(8,128)(2,1)S(1)}, u32[]{:S(2)}, u32[]{:S(2)}) async-start(bf16[64,1,64,128]{3,2,1,0:T(8,128)(2,1)} %bitcast.198), calls=%async_computation.3 | async-start | bytes 2097152 | tf_op jit(solution)/shard_map/all_to_all | solution.py:138
  223.2 0.0 reduce-scatter.5.cloned.1.call-start
  223.2 0.1 broadcast_in_dim.86
  223.3 0.1 broadcast_in_dim.87
  223.4 28.5 %all-to-all-done.2 = bf16[64,1,64,128]{3,2,1,0:T(8,128)(2,1)S(1)} async-done(((bf16[64,1,64,128]{3,2,1,0:T(8,128)(2,1)}), bf16[64,1,64,128]{3,2,1,0:T(8,128)(2,1)S(1)}, u32[]{:S(2)}, u32[]{:S(2)}) %all-to-all-start.2) | async-done | bytes 1048608 | tf_op jit(solution)/shard_map/all_to_all | solution.py:138
  251.9 0.2 bitcast_convert_fusion
  252.2 3.8 %scatter_fusion = f32[9,64,128]{2,1,0:T(8,128)S(1)} fusion(f32[9,64,128]{2,1,0:T(8,128)S(1)} %broadcast_in_dim.89, s32[64]{0:T(128)S(1)} %fusion.53, f32[64,64,128]{2,1,0:T(8,128)S(1)} %bitcast_convert_fusion), kind=kCustom, calls=%fused_computation.5 | custom fusion | flops 524288 | bytes 6291712 | tf_op jit(solution)/shard_map/scatter-add | solution.py:149
  256.0 0.1 broadcast_in_dim.92
  256.1 2.3 fusion.32
  258.4 3.8 %fusion.30 = bf16[8,128,2,128]{1,3,2,0:T(8,128)(2,1)S(1)} fusion(bf16[8,2,128,8,128]{2,4,1,3,0:T(8,128)(2,1)} %fusion.1, bf16[8,8,2,128,128]{4,3,1,0,2:T(8,128)(2,1)} %bitcast.189), kind=kOutput, calls=%fused_computation.42 | convolution fusion | flops 537395200 | bytes 6815744 | tf_op jit(solution)/shard_map/qhisj,qsjd->qihd/dot_general | solution.py:109
  262.2 0.4 copy.125
  262.6 0.4 copy.116
  263.0 1.1 copy_bitcast_fusion.1
  264.2 13.5 %reduce-scatter.5.cloned.1.call-done = bf16[2,256,128]{2,1,0:T(8,128)(2,1)} async-done(((bf16[2,1024,128]{2,1,0:T(8,128)(2,1)}), bf16[2,256,128]{2,1,0:T(8,128)(2,1)}) %reduce-scatter.5.cloned.1.call-update) | async-done | bytes 131088 | tf_op jit(solution)/shard_map/reduce_scatter | solution.py:155
  277.6 1.5 slice_bitcast_fusion.18
  (42 shorter events, 0.4 us)
Async XLA Ops:
  7.2 63.3 %copy-start.5 = (bf16[1024,256]{1,0:T(8,128)(2,1)S(1)}, bf16[1024,256]{1,0:T(8,128)(2,1)}, u32[]{:S(2)}) copy-start(bf16[1024,256]{1,0:T(8,128)(2,1)} %param.5) | copy-start | bytes 1572868
  7.2 63.6 %copy-start.6 = (bf16[1024,256]{1,0:T(8,128)(2,1)S(1)}, bf16[1024,256]{1,0:T(8,128)(2,1)}, u32[]{:S(2)}) copy-start(bf16[1024,256]{1,0:T(8,128)(2,1)} %param.8) | copy-start | bytes 1572868
  12.1 20.7 %all-to-all-start = ((s32[64,1,1]{2,1,0:T(1,128)}), s32[64,1,1]{2,1,0:T(1,128)S(1)}, u32[]{:S(2)}, u32[]{:S(2)}) async-start(s32[64,1,1]{2,1,0:T(1,128)} %copy.76), calls=%async_computation | async-start | bytes 65536 | tf_op jit(solution)/shard_map/all_to_all | solution.py:49
  24.2 93.5 %all-gather.3.cloned.1.call-start = ((), (), s32[]{:S(2)}) async-start(), calls=%async_computation.7 | async-start | bytes 5242880 | tf_op jit(solution)/shard_map/all_gather | solution.py:60
  35.2 37.2 %copy-start.8 = (s32[8,8]{1,0:T(8,128)S(1)}, s32[8,8]{1,0:T(8,128)}, u32[]{:S(2)}) copy-start(s32[8,8]{1,0:T(8,128)} %param.9) | copy-start | bytes 772
  35.9 81.8 %copy-start.3 = (bf16[1024,128]{1,0:T(8,128)(2,1)S(1)}, bf16[1024,128]{1,0:T(8,128)(2,1)}, u32[]{:S(2)}) copy-start(bf16[1024,128]{1,0:T(8,128)(2,1)} %param.7) | copy-start | bytes 786436
  36.0 81.8 %copy-start.4 = (bf16[1024,128]{1,0:T(8,128)(2,1)S(1)}, bf16[1024,128]{1,0:T(8,128)(2,1)}, u32[]{:S(2)}) copy-start(bf16[1024,128]{1,0:T(8,128)(2,1)} %param.6) | copy-start | bytes 786436
  70.4 142.2 %reduce-scatter.3.cloned.1.call-start = ((), (), s32[]{:S(2)}) async-start(), calls=%async_computation.5 | async-start | bytes 5242880 | tf_op jit(solution)/shard_map/reduce_scatter | solution.py:135
  129.7 9.2 %copy-start.2 = (bf16[64,2,128,128]{3,2,0,1:T(8,128)(2,1)}, bf16[64,2,128,128]{3,2,0,1:T(8,128)(2,1)S(1)}, u32[]{:S(2)}) copy-start(bf16[64,2,128,128]{3,2,0,1:T(8,128)(2,1)S(1)} %copy.77) | copy-start | bytes 12582916
  138.9 7.7 %copy-start.1 = (f32[8,8,1,128,128]{4,3,1,0,2:T(8,128)}, f32[8,8,1,128,128]{4,3,1,0,2:T(8,128)S(1)}, u32[]{:S(2)}) copy-start(f32[8,8,1,128,128]{4,3,1,0,2:T(8,128)S(1)} %fusion.19) | copy-start | bytes 12582916
  146.6 2.0 copy-start
  212.6 39.3 %all-to-all-start.2 = ((bf16[64,1,64,128]{3,2,1,0:T(8,128)(2,1)}), bf16[64,1,64,128]{3,2,1,0:T(8,128)(2,1)S(1)}, u32[]{:S(2)}, u32[]{:S(2)}) async-start(bf16[64,1,64,128]{3,2,1,0:T(8,128)(2,1)} %bitcast.198), calls=%async_computation.3 | async-start | bytes 2097152 | tf_op jit(solution)/shard_map/all_to_all | solution.py:138
  223.2 54.5 %reduce-scatter.5.cloned.1.call-start = ((), (), s32[]{:S(2)}) async-start(), calls=%async_computation.6 | async-start | bytes 655360 | tf_op jit(solution)/shard_map/reduce_scatter | solution.py:155
  258.4 4.2 %copy-start.7 = (bf16[8,128,2,128]{1,3,2,0:T(8,128)(2,1)S(1)}, bf16[8,128,2,128]{1,3,2,0:T(8,128)(2,1)}, u32[]{:S(2)}) copy-start(bf16[8,128,2,128]{1,3,2,0:T(8,128)(2,1)} %get-tuple-element.35) | copy-start | bytes 1572868
Sparse Core Ops, SparseCore 0:
  70.5 47.2 all-gather.2
  162.8 49.7 reduce-scatter.2
  258.5 19.0 reduce-scatter.4

commit v2 on v1

--- a/solution.py
+++ b/solution.py
@@ -34,6 +34,24 @@
     return (owner_dev, local_blk, rank_in, usable)
 
 
+def head_shift(x, shift, count):
+    return lax.ppermute(x, "head", [(j, (j + shift) % count) for j in range(count)])
+
+
+def head_gather(part, head_idx, count):
+    by_shift = jnp.stack([part] + [head_shift(part, k, count) for k in range(1, count)])
+    order = (head_idx - jnp.arange(count, dtype=jnp.int32)) % count
+    return by_shift[order]
+
+
+def head_reduce(parts, head_idx, count):
+    total = lax.dynamic_index_in_dim(parts, head_idx, axis=0, keepdims=False).astype(jnp.float32)
+    for k in range(1, count):
+        piece = lax.dynamic_index_in_dim(parts, (head_idx + k) % count, axis=0, keepdims=False)
+        total = total + head_shift(piece, k, count).astype(jnp.float32)
+    return total
+
+
 def on_device(queries, key_rows, value_rows, out_grad, block_lists):
     pair_count = lax.axis_size("ctx")
     half_blocks = QB // 2
@@ -57,7 +75,7 @@
     my_part = lax.dynamic_index_in_dim(kv_parts, head_idx, axis=1, keepdims=False)
     send_parts = my_part[jnp.maximum(requested, 0)]
     fetched_part = lax.all_to_all(send_parts, "ctx", split_axis=0, concat_axis=0, tiled=True)
-    fetched = lax.all_gather(fetched_part, "head", axis=2, tiled=False)
+    fetched = jnp.moveaxis(head_gather(fetched_part, head_idx, head_count), 0, 2)
     kv_table = jnp.concatenate([kv_blocks, fetched.reshape(total_slots, 2, BLK, HD)], axis=0)
     local_ids = jnp.arange(QB, dtype=jnp.int32)
     remote_idx = jnp.where(usable, QB + slot_idx, 0).reshape(QB, SEL - 1)
@@ -132,9 +150,7 @@
     )
     remote_parts = jnp.moveaxis(remote_tiles.reshape(entry_count + 1, head_count, part_rows, HD), 1, 0)
     outgoing = remote_parts[:, slot_entry].astype(jnp.bfloat16)
-    outgoing_part = lax.psum_scatter(
-        outgoing.reshape(head_count * total_slots * part_rows, HD), "head", scatter_dimension=0, tiled=True
-    )
+    outgoing_part = head_reduce(outgoing, head_idx, head_count).astype(jnp.bfloat16)
     returned = lax.all_to_all(
         outgoing_part.reshape(pair_count, capacity, part_rows, HD),
         "ctx",
@@ -151,10 +167,8 @@
     own_parts = grad_tiles[:, 0].reshape(QB, head_count, part_rows, HD)
     mine = (jnp.arange(head_count, dtype=jnp.int32) == head_idx)[None, :, None, None]
     own_parts = own_parts + jnp.where(mine, returned_sum[:, None], 0.0)
-    combined = jnp.transpose(own_parts.reshape(QB, 2, BLK, HD), (1, 0, 2, 3)).reshape(2, QB * BLK, HD)
-    reduced = lax.psum_scatter(
-        combined.astype(jnp.bfloat16), "head", scatter_dimension=1, tiled=True
-    ).astype(jnp.float32)
+    combined = jnp.transpose(own_parts.reshape(head_count, QB // head_count, 2, BLK, HD), (0, 2, 1, 3, 4))
+    reduced = head_reduce(combined.astype(jnp.bfloat16), head_idx, head_count).reshape(2, -1, HD)
     return (
         attended.reshape(QB * BLK, heads_here * HD),
         query_grad.reshape(QB * BLK, heads_here * HD),

time: 286 us -> 270 us (0.944)
  blocking collectives: 34.4 us -> 0 us
  between operations: 14.2 us -> 1.18 us
  starting transfers between devices: 22.8 us -> 33 us
  local copies, waits for them, and re-layouts: 31.7 us -> 39.7 us
  waiting for transfers between devices: 143 us -> 151 us
  other arithmetic: 21.1 us -> 25.2 us
    ppermute x0 -> x9, waiting for transfers between devices: none -> 97.3 us  [head_shift(): lax.ppermute(x, 'head', [(j, (j + shift) % count) for j in range(count)])]
    reduce_scatter x2 -> x0, waiting for transfers between devices: 63.4 us -> none  [the longest x1 49.9 us: on_device(): lax.psum_scatter(outgoing.reshape(head_count * total_slots * part_rows, H...]
    all_gather x1 -> x0, waiting for transfers between devices: 43.8 us -> none  [on_device(): fetched = lax.all_gather(fetched_part, 'head', axis=2, tiled=False)]
    all_to_all x1 -> x0, blocking collectives: 34.4 us -> none  [on_device(): lax.all_to_all(send_parts, 'ctx', split_axis=0, concat_axis=0, tiled=True)]
    all_to_all x0 -> x1, waiting for transfers between devices: none -> 26.4 us  [on_device(): lax.all_to_all(send_parts, 'ctx', split_axis=0, concat_axis=0, tiled=True)]
    ppermute x0 -> x9, starting transfers between devices: none -> 9.03 us  [head_shift(): lax.ppermute(x, 'head', [(j, (j + shift) % count) for j in range(count)])]
    all_to_all x1, waiting for transfers between devices: 28.5 us -> 20.3 us  [on_device(): lax.all_to_all(outgoing_part.reshape(pair_count, capacity, part_rows, HD)...]
    convert_element_type x2 -> x0, local copies, waits for them, and re-layouts: 6.98 us -> none  [the longest x1 5.45 us: on_device(): outgoing = remote_parts[:, slot_entry].astype(jnp.bfloat16)]
  transfers between devices with their start and end apart: 5 -> 12, of which waited for: 5 -> 11; matrix products, arithmetic and copies ran while one was open for 4% -> 5% of each run, Pallas kernels for 0% -> 0%
where the time goes in v2:
time: 270 us; the launch traced here: 268 us
  waiting for transfers between devices  151 us (56%)
  local copies, waits for them, and re-layouts  39.7 us (15%)
  starting transfers between devices  33 us (12%)
  other arithmetic  25.2 us (9%)
  matrix products  17.6 us (7%)
    ppermute x9, waiting for transfers between devices, head_shift(): lax.ppermute(x, 'head', [(j, (j + shift) % count) for j in range(count)])  97.3 us
    all_to_all x1, waiting for transfers between devices, on_device(): lax.all_to_all(send_parts, 'ctx', split_axis=0, concat_axis=0, tiled=True)  26.4 us
    all_to_all x1, waiting for transfers between devices, on_device(): lax.all_to_all(outgoing_part.reshape(pair_count, capacity, part_rows, HD)...  20.3 us
    all_to_all x1, starting transfers between devices, on_device(): lax.all_to_all(req_table.reshape(pair_count, capacity), 'ctx', split_axis...  12.1 us
    ppermute x9, starting transfers between devices, head_shift(): lax.ppermute(x, 'head', [(j, (j + shift) % count) for j in range(count)])  9.03 us
    gather x2, local copies, waits for them, and re-layouts, on_device(): kv_tiles = kv_table[entry_idx]  7.95 us
    all_to_all x1, waiting for transfers between devices, on_device(): lax.all_to_all(req_table.reshape(pair_count, capacity), 'ctx', split_axis...  7.41 us
    all_to_all x1, starting transfers between devices, on_device(): lax.all_to_all(outgoing_part.reshape(pair_count, capacity, part_rows, HD)...  6.36 us
  transfers between devices with their start and end apart: 12, of which 11 were waited for; matrix products, arithmetic and copies ran while one was open for 5% of the time, Pallas kernels for 0%

profile of v2, /device:TPU:8, one launch (start us, length us, event | category | flops | bytes accessed | tf_op | source)
XLA Modules:
  0.0 268.1 jit_solution(3759156486861192175)
XLA Ops:
  0.6 0.8 sign_compare_fusion
  1.5 0.8 fusion.52
  2.9 0.2 select_reduce_fusion
  3.2 0.8 fusion.51
  4.1 0.7 scatter_custom_fusion
  4.9 0.7 copy.85
  5.6 12.1 %all-to-all-start = ((s32[64,1,1]{2,1,0:T(1,128)}), s32[64,1,1]{2,1,0:T(1,128)S(1)}, u32[]{:S(2)}, u32[]{:S(2)}) async-start(s32[64,1,1]{2,1,0:T(1,128)} %copy.85), calls=%async_computation | async-start | bytes 65536 | tf_op jit(solution)/shard_map/all_to_all | solution.py:67
  17.7 1.1 pad_maximum_fusion.3
  18.8 7.4 %all-to-all-done = s32[64,1,1]{2,1,0:T(1,128)S(1)} async-done(((s32[64,1,1]{2,1,0:T(1,128)}), s32[64,1,1]{2,1,0:T(1,128)S(1)}, u32[]{:S(2)}, u32[]{:S(2)}) %all-to-all-start) | async-done | bytes 288 | tf_op jit(solution)/shard_map/all_to_all | solution.py:67
  26.2 2.4 fusion.70
  28.6 1.7 gather_fusion
  30.3 5.5 %all-to-all-start.1 = ((bf16[64,1,64,128]{3,2,1,0:T(8,128)(2,1)}), bf16[64,1,64,128]{3,2,1,0:T(8,128)(2,1)S(1)}, u32[]{:S(2)}, u32[]{:S(2)}) async-start(bf16[64,1,64,128]{3,2,1,0:T(8,128)(2,1)} %bitcast.7), calls=%async_computation.1 | async-start | bytes 2097152 | tf_op jit(solution)/shard_map/all_to_all | solution.py:77
  36.3 1.1 copy.97
  37.4 0.7 scatter_custom_fusion.1
  38.3 26.4 %all-to-all-done.1 = bf16[64,1,64,128]{3,2,1,0:T(8,128)(2,1)S(1)} async-done(((bf16[64,1,64,128]{3,2,1,0:T(8,128)(2,1)}), bf16[64,1,64,128]{3,2,1,0:T(8,128)(2,1)S(1)}, u32[]{:S(2)}, u32[]{:S(2)}) %all-to-all-start.1) | async-done | bytes 1048608 | tf_op jit(solution)/shard_map/all_to_all | solution.py:77
  64.7 2.8 %collective-permute-start.2 = (bf16[64,1,64,128]{3,2,0,1:T(8,128)(2,1)S(1)}, bf16[64,1,64,128]{3,2,0,1:T(8,128)(2,1)S(1)}, u32[]{:S(2)}, u32[]{:S(2)}) collective-permute-start(bf16[64,1,64,128]{3,2,0,1:T(8,128)(2,1)S(1)} %bitcast.222), channel_id=1, source_target_pairs={{0,3},{1,0},{2,1},{3,2},{4,7},{5,4},{6,5},{7,6},{8,11},{9,8},{10,9... | collective-permute-start | bytes 3145736 | tf_op jit(solution)/shard_map/ppermute | solution.py:38
  67.5 0.8 collective-permute-start.1
  68.3 0.9 collective-permute-start
  69.2 1.5 compare_and_fusion
  70.7 40.7 %collective-permute-done.2 = bf16[64,1,64,128]{3,2,0,1:T(8,128)(2,1)S(1)} collective-permute-done((bf16[64,1,64,128]{3,2,0,1:T(8,128)(2,1)S(1)}, bf16[64,1,64,128]{3,2,0,1:T(8,128)(2,1)S(1)}, u32[]{:S(2)}, u32[]{:S(2)}) %collective-permute-start.2) | collective-permute-done | bytes 1048608 | tf_op jit(solution)/shard_map/ppermute | solution.py:38
  111.4 3.7 %collective-permute-done = bf16[64,1,64,128]{3,2,0,1:T(8,128)(2,1)S(1)} collective-permute-done((bf16[64,1,64,128]{3,2,0,1:T(8,128)(2,1)S(1)}, bf16[64,1,64,128]{3,2,0,1:T(8,128)(2,1)S(1)}, u32[]{:S(2)}, u32[]{:S(2)}) %collective-permute-start) | collective-permute-done | bytes 1048608 | tf_op jit(solution)/shard_map/ppermute | solution.py:38
  115.1 2.2 maximum_bitcast_fusion
  117.3 5.2 %gather_fusion.1 = bf16[4,64,64,128]{3,2,1,0:T(8,128)(2,1)} fusion(bf16[4,64,64,128]{3,2,1,0:T(8,128)(2,1)} %maximum_bitcast_fusion, s32[1024]{0:T(1024)S(1)} %pad_clamp_fusion.2), kind=kCustom, calls=%fused_computation.1 | custom fusion | bytes 8388624 | tf_op jit(solution)/shard_map/gather | solution.py:44
  122.5 3.6 %copy.89 = bf16[64,1,4,64,128]{4,3,2,0,1:T(8,128)(2,1)S(1)} copy(bf16[64,1,4,64,128]{4,3,0,2,1:T(8,128)(2,1)} %bitcast.212) | data formatting | bytes 8388608 | tf_op jit(solution)/shard_map/transpose | solution.py:78
  126.2 2.4 pad_maximum_fusion.1
  128.5 5.5 %gather_fusion.2 = bf16[64,2,128,128]{3,2,1,0:T(8,128)(2,1)} fusion(bf16[72,2,128,128]{3,2,1,0:T(8,128)(2,1)} %pad_maximum_fusion.1, s32[1024]{0:T(1024)S(1)} %pad_clamp_fusion.1), kind=kCustom, calls=%fused_computation.2 | custom fusion | bytes 8388864 | tf_op jit(solution)/shard_map/gather | solution.py:83
  134.0 2.5 copy.90
  136.5 1.5 fusion.5
  138.1 2.2 fusion.2
  140.3 2.6 multiply_reduce_fusion
  142.9 2.2 fusion.19
  145.1 4.2 %fusion.1 = bf16[8,2,128,8,128]{2,4,1,3,0:T(8,128)(2,1)} fusion(f32[8,8,128,128,2]{3,2,4,1,0:T(8,128)S(1)} %get-tuple-element.39, f32[8,2,128]{2,1,0:T(2,128)S(1)} %bitcast.247, f32[8,2,128]{2,1,0:T(2,128)S(1)} %bitcast.246, pred[8,128,8,128]{1,3,2,0:T(8,128)(4,1)S(1)} %compare_and_fusion, bf16[8,8,2,128,128]{4,3,1,0,2:T(8,128)(2,1)S(1)} %bitcast.220, ...), kind=kOutput, calls=%fused_computation.9 | convolution fusion | flops 549453824 | bytes 16269312 | tf_op jit(solution)/shard_map/qihd,qsjd->qhisj/dot_general | solution.py:120
  149.2 3.4 %fusion.10 = f32[8,8,1,128,128]{4,3,1,0,2:T(8,128)S(1)} fusion(bf16[8,2,128,8,128]{2,4,1,3,0:T(8,128)(2,1)} %fusion.1, bf16[8,128,2,128,1]{3,2,1,0,4:T(2,128)(2,1)S(1)} %bitcast.227), kind=kOutput, calls=%fused_computation.24 | convolution fusion | flops 537919488 | bytes 8912896 | tf_op jit(solution)/shard_map/qhisj,qihd->qsjd/dot_general | solution.py:131
  152.7 0.7 pad_maximum_fusion
  153.4 1.2 copy-done
  154.7 0.4 copy.103
  155.1 0.5 concatenate.33
  155.6 2.7 copy.163
  158.3 5.1 %gather_fusion.3 = bf16[64,4,64,128]{3,2,1,0:T(8,128)(2,1)} fusion(bf16[4,57,64,128]{3,2,1,0:T(8,128)(2,1)} %bitcast.211, s32[1024]{0:T(1024)S(1)} %pad_clamp_fusion), kind=kCustom, calls=%fused_computation.3 | custom fusion | bytes 8388864 | tf_op jit(solution)/shard_map/gather | solution.py:152
  163.4 2.6 dynamic-slice_bitcast_fusion.2
  165.9 0.7 collective-permute-start.5
  166.6 0.8 collective-permute-start.4
  167.4 0.8 collective-permute-start.3
  168.2 23.8 %collective-permute-done.5 = bf16[64,64,128]{2,1,0:T(8,128)(2,1)S(1)} collective-permute-done((bf16[64,64,128]{2,1,0:T(8,128)(2,1)S(1)}, bf16[64,64,128]{2,1,0:T(8,128)(2,1)S(1)}, u32[]{:S(2)}, u32[]{:S(2)}) %collective-permute-start.5) | collective-permute-done | bytes 1048608 | tf_op jit(solution)/shard_map/ppermute | solution.py:38
  192.0 2.2 collective-permute-done.4
  194.2 21.0 %collective-permute-done.3 = bf16[64,64,128]{2,1,0:T(8,128)(2,1)S(1)} collective-permute-done((bf16[64,64,128]{2,1,0:T(8,128)(2,1)S(1)}, bf16[64,64,128]{2,1,0:T(8,128)(2,1)S(1)}, u32[]{:S(2)}, u32[]{:S(2)}) %collective-permute-start.3) | collective-permute-done | bytes 1048608 | tf_op jit(solution)/shard_map/ppermute | solution.py:38
  215.1 3.1 %fusion.34 = bf16[64,1,64,128]{3,2,1,0:T(8,128)(2,1)} fusion(bf16[64,64,128]{2,1,0:T(8,128)(2,1)S(1)} %collective-permute-done.5, bf16[64,64,128]{2,1,0:T(8,128)(2,1)S(1)} %collective-permute-done.4, bf16[64,64,128]{2,1,0:T(8,128)(2,1)S(1)} %collective-permute-done.3, bf16[64,4,64,128]{3,2,1,0:T(8,128)(2,1)} %gather_fusion.3, s32[]{:T(128)S(6)} %select_n.196), kind=kLoop, calls=%fused_computation.48 | loop fusion | flops 4194304 | bytes 5242884 | tf_op jit(solution)/shard_map/reshape | solution.py:155
  218.2 6.4 %all-to-all-start.2 = ((bf16[64,1,64,128]{3,2,1,0:T(8,128)(2,1)}), bf16[64,1,64,128]{3,2,1,0:T(8,128)(2,1)S(1)}, u32[]{:S(2)}, u32[]{:S(2)}) async-start(bf16[64,1,64,128]{3,2,1,0:T(8,128)(2,1)} %fusion.34), calls=%async_computation.2 | async-start | bytes 2097152 | tf_op jit(solution)/shard_map/all_to_all | solution.py:154
  224.8 3.7 %fusion.33 = bf16[8,128,2,128]{1,3,2,0:T(8,128)(2,1)S(1)} fusion(bf16[8,2,128,8,128]{2,4,1,3,0:T(8,128)(2,1)} %fusion.1, bf16[8,8,2,128,128]{4,3,1,0,2:T(8,128)(2,1)} %bitcast.221), kind=kOutput, calls=%fused_computation.47 | convolution fusion | flops 537395200 | bytes 6815744 | tf_op jit(solution)/shard_map/qhisj,qsjd->qihd/dot_general | solution.py:127
  228.5 1.1 copy.137
  229.6 1.1 copy.128
  230.7 2.4 pad_maximum_fusion.2
  233.1 20.3 %all-to-all-done.2 = bf16[64,1,64,128]{3,2,1,0:T(8,128)(2,1)S(1)} async-done(((bf16[64,1,64,128]{3,2,1,0:T(8,128)(2,1)}), bf16[64,1,64,128]{3,2,1,0:T(8,128)(2,1)S(1)}, u32[]{:S(2)}, u32[]{:S(2)}) %all-to-all-start.2) | async-done | bytes 1048608 | tf_op jit(solution)/shard_map/all_to_all | solution.py:154
  253.3 0.2 bitcast_convert_fusion
  253.6 3.8 %scatter_fusion = f32[9,64,128]{2,1,0:T(8,128)S(1)} fusion(f32[9,64,128]{2,1,0:T(8,128)S(1)} %broadcast_in_dim.90, s32[64]{0:T(128)S(1)} %fusion.61, f32[64,64,128]{2,1,0:T(8,128)S(1)} %bitcast_convert_fusion), kind=kCustom, calls=%fused_computation.6 | custom fusion | flops 524288 | bytes 6291712 | tf_op jit(solution)/shard_map/scatter-add | solution.py:165
  257.6 0.2 fusion.35
  257.9 1.1 collective-permute-start.8
  259.0 0.3 collective-permute-start.7
  259.4 0.8 collective-permute-start.6
  260.2 1.1 copy_bitcast_fusion.1
  261.3 2.3 collective-permute-done.8
  263.6 2.3 collective-permute-done.7
  265.9 1.4 collective-permute-done.6
  267.4 0.7 fusion.71
  (67 shorter events, 2.0 us)
Async XLA Ops:
  0.6 35.2 %copy-start.8 = (bf16[1024,256]{1,0:T(8,128)(2,1)S(1)}, bf16[1024,256]{1,0:T(8,128)(2,1)}, u32[]{:S(2)}) copy-start(bf16[1024,256]{1,0:T(8,128)(2,1)} %param.5) | copy-start | bytes 1572868
  5.6 20.7 %all-to-all-start = ((s32[64,1,1]{2,1,0:T(1,128)}), s32[64,1,1]{2,1,0:T(1,128)S(1)}, u32[]{:S(2)}, u32[]{:S(2)}) async-start(s32[64,1,1]{2,1,0:T(1,128)} %copy.85), calls=%async_computation | async-start | bytes 65536 | tf_op jit(solution)/shard_map/all_to_all | solution.py:67
  17.7 51.5 %copy-start.11 = (s32[8,8]{1,0:T(8,128)S(1)}, s32[8,8]{1,0:T(8,128)}, u32[]{:S(2)}) copy-start(s32[8,8]{1,0:T(8,128)} %param.9) | copy-start | bytes 772
  18.8 17.4 %copy-start.9 = (bf16[1024,256]{1,0:T(8,128)(2,1)S(1)}, bf16[1024,256]{1,0:T(8,128)(2,1)}, u32[]{:S(2)}) copy-start(bf16[1024,256]{1,0:T(8,128)(2,1)} %param.8) | copy-start | bytes 1572868
  30.3 34.4 %all-to-all-start.1 = ((bf16[64,1,64,128]{3,2,1,0:T(8,128)(2,1)}), bf16[64,1,64,128]{3,2,1,0:T(8,128)(2,1)S(1)}, u32[]{:S(2)}, u32[]{:S(2)}) async-start(bf16[64,1,64,128]{3,2,1,0:T(8,128)(2,1)} %bitcast.7), calls=%async_computation.1 | async-start | bytes 2097152 | tf_op jit(solution)/shard_map/all_to_all | solution.py:77
  64.7 46.7 %collective-permute-start.2 = (bf16[64,1,64,128]{3,2,0,1:T(8,128)(2,1)S(1)}, bf16[64,1,64,128]{3,2,0,1:T(8,128)(2,1)S(1)}, u32[]{:S(2)}, u32[]{:S(2)}) collective-permute-start(bf16[64,1,64,128]{3,2,0,1:T(8,128)(2,1)S(1)} %bitcast.222), channel_id=1, source_target_pairs={{0,3},{1,0},{2,1},{3,2},{4,7},{5,4},{6,5},{7,6},{8,11},{9,8},{10,9... | collective-permute-start | bytes 3145736 | tf_op jit(solution)/shard_map/ppermute | solution.py:38
  67.5 44.0 %collective-permute-start.1 = (bf16[64,1,64,128]{3,2,0,1:T(8,128)(2,1)S(1)}, bf16[64,1,64,128]{3,2,0,1:T(8,128)(2,1)S(1)}, u32[]{:S(2)}, u32[]{:S(2)}) collective-permute-start(bf16[64,1,64,128]{3,2,0,1:T(8,128)(2,1)S(1)} %bitcast.223), channel_id=1, source_target_pairs={{0,2},{1,3},{2,0},{3,1},{4,6},{5,7},{6,4},{7,5},{8,10},{9,11},{10,... | collective-permute-start | bytes 3145736 | tf_op jit(solution)/shard_map/ppermute | solution.py:38
  68.3 46.8 %collective-permute-start = (bf16[64,1,64,128]{3,2,0,1:T(8,128)(2,1)S(1)}, bf16[64,1,64,128]{3,2,0,1:T(8,128)(2,1)S(1)}, u32[]{:S(2)}, u32[]{:S(2)}) collective-permute-start(bf16[64,1,64,128]{3,2,0,1:T(8,128)(2,1)S(1)} %bitcast.224), channel_id=1, source_target_pairs={{0,1},{1,2},{2,3},{3,0},{4,5},{5,6},{6,7},{7,4},{8,9},{9,10},{10,1... | collective-permute-start | bytes 3145736 | tf_op jit(solution)/shard_map/ppermute | solution.py:38
  122.5 3.7 %copy-start.6 = (bf16[1024,128]{1,0:T(8,128)(2,1)S(1)}, bf16[1024,128]{1,0:T(8,128)(2,1)}, u32[]{:S(2)}) copy-start(bf16[1024,128]{1,0:T(8,128)(2,1)} %param.7) | copy-start | bytes 786436
  122.5 3.7 %copy-start.7 = (bf16[1024,128]{1,0:T(8,128)(2,1)S(1)}, bf16[1024,128]{1,0:T(8,128)(2,1)}, u32[]{:S(2)}) copy-start(bf16[1024,128]{1,0:T(8,128)(2,1)} %param.6) | copy-start | bytes 786436
  136.5 8.6 %copy-start.3 = (bf16[64,2,128,128]{3,2,0,1:T(8,128)(2,1)}, bf16[64,2,128,128]{3,2,0,1:T(8,128)(2,1)S(1)}, u32[]{:S(2)}) copy-start(bf16[64,2,128,128]{3,2,0,1:T(8,128)(2,1)S(1)} %copy.90) | copy-start | bytes 12582916
  138.1 2.2 copy-start.10
  145.1 7.6 %copy-start.1 = (f32[8,8,1,128,128]{4,3,1,0,2:T(8,128)}, f32[8,8,1,128,128]{4,3,1,0,2:T(8,128)S(1)}, u32[]{:S(2)}) copy-start(f32[8,8,1,128,128]{4,3,1,0,2:T(8,128)S(1)} %fusion.19) | copy-start | bytes 12582916
  152.7 2.0 copy-start
  165.9 26.1 %collective-permute-start.5 = (bf16[64,64,128]{2,1,0:T(8,128)(2,1)S(1)}, bf16[64,64,128]{2,1,0:T(8,128)(2,1)S(1)}, u32[]{:S(2)}, u32[]{:S(2)}) collective-permute-start(bf16[64,64,128]{2,1,0:T(8,128)(2,1)S(1)} %get-tuple-element.27), channel_id=1, source_target_pairs={{0,3},{1,0},{2,1},{3,2},{4,7},{5,4},{6,5},{7,6},{8,11},{9,8},{10,9... | collective-permute-start | bytes 3145736 | tf_op jit(solution)/shard_map/ppermute | solution.py:38
  166.6 27.6 %collective-permute-start.4 = (bf16[64,64,128]{2,1,0:T(8,128)(2,1)S(1)}, bf16[64,64,128]{2,1,0:T(8,128)(2,1)S(1)}, u32[]{:S(2)}, u32[]{:S(2)}) collective-permute-start(bf16[64,64,128]{2,1,0:T(8,128)(2,1)S(1)} %get-tuple-element.28), channel_id=1, source_target_pairs={{0,2},{1,3},{2,0},{3,1},{4,6},{5,7},{6,4},{7,5},{8,10},{9,11},{10,... | collective-permute-start | bytes 3145736 | tf_op jit(solution)/shard_map/ppermute | solution.py:38
  167.4 47.7 %collective-permute-start.3 = (bf16[64,64,128]{2,1,0:T(8,128)(2,1)S(1)}, bf16[64,64,128]{2,1,0:T(8,128)(2,1)S(1)}, u32[]{:S(2)}, u32[]{:S(2)}) collective-permute-start(bf16[64,64,128]{2,1,0:T(8,128)(2,1)S(1)} %get-tuple-element.26), channel_id=1, source_target_pairs={{0,1},{1,2},{2,3},{3,0},{4,5},{5,6},{6,7},{7,4},{8,9},{9,10},{10,1... | collective-permute-start | bytes 3145736 | tf_op jit(solution)/shard_map/ppermute | solution.py:38
  218.2 35.1 %all-to-all-start.2 = ((bf16[64,1,64,128]{3,2,1,0:T(8,128)(2,1)}), bf16[64,1,64,128]{3,2,1,0:T(8,128)(2,1)S(1)}, u32[]{:S(2)}, u32[]{:S(2)}) async-start(bf16[64,1,64,128]{3,2,1,0:T(8,128)(2,1)} %fusion.34), calls=%async_computation.2 | async-start | bytes 2097152 | tf_op jit(solution)/shard_map/all_to_all | solution.py:154
  253.6 4.0 %copy-start.2 = (f32[8,1,2,128,128]{4,3,1,0,2:T(8,128)S(1)}, f32[8,1,2,128,128]{4,3,1,0,2:T(8,128)}, u32[]{:S(2)}) copy-start(f32[8,1,2,128,128]{4,3,1,0,2:T(8,128)} %pad_maximum_fusion.2) | copy-start | bytes 3145732
  257.4 2.8 %copy-start.4 = (bf16[8,128,2,128]{3,2,1,0:T(2,128)(2,1)S(1)}, bf16[8,128,2,128]{3,2,1,0:T(2,128)(2,1)}, u32[]{:S(2)}) copy-start(bf16[8,128,2,128]{3,2,1,0:T(2,128)(2,1)} %copy.137) | copy-start | bytes 1572868
  257.4 2.8 %copy-start.5 = (bf16[8,128,2,128]{3,2,1,0:T(2,128)(2,1)S(1)}, bf16[8,128,2,128]{3,2,1,0:T(2,128)(2,1)}, u32[]{:S(2)}) copy-start(bf16[8,128,2,128]{3,2,1,0:T(2,128)(2,1)} %copy.128) | copy-start | bytes 1572868
  257.9 5.7 %collective-permute-start.8 = (bf16[2,2,128,128]{3,2,0,1:T(8,128)(2,1)S(1)}, bf16[2,2,128,128]{3,2,0,1:T(8,128)(2,1)S(1)}, u32[]{:S(2)}, u32[]{:S(2)}) collective-permute-start(bf16[2,2,128,128]{3,2,0,1:T(8,128)(2,1)S(1)} %get-tuple-element.30), channel_id=1, source_target_pairs={{0,3},{1,0},{2,1},{3,2},{4,7},{5,4},{6,5},{7,6},{8,11},{9,8},{10,9... | collective-permute-start | bytes 393224 | tf_op jit(solution)/shard_map/ppermute | solution.py:38
  259.0 6.9 %collective-permute-start.7 = (bf16[2,2,128,128]{3,2,0,1:T(8,128)(2,1)S(1)}, bf16[2,2,128,128]{3,2,0,1:T(8,128)(2,1)S(1)}, u32[]{:S(2)}, u32[]{:S(2)}) collective-permute-start(bf16[2,2,128,128]{3,2,0,1:T(8,128)(2,1)S(1)} %get-tuple-element.31), channel_id=1, source_target_pairs={{0,2},{1,3},{2,0},{3,1},{4,6},{5,7},{6,4},{7,5},{8,10},{9,11},{10,... | collective-permute-start | bytes 393224 | tf_op jit(solution)/shard_map/ppermute | solution.py:38
  259.4 8.0 %collective-permute-start.6 = (bf16[2,2,128,128]{3,2,0,1:T(8,128)(2,1)S(1)}, bf16[2,2,128,128]{3,2,0,1:T(8,128)(2,1)S(1)}, u32[]{:S(2)}, u32[]{:S(2)}) collective-permute-start(bf16[2,2,128,128]{3,2,0,1:T(8,128)(2,1)S(1)} %get-tuple-element.29), channel_id=1, source_target_pairs={{0,1},{1,2},{2,3},{3,0},{4,5},{5,6},{6,7},{7,4},{8,9},{9,10},{10,1... | collective-permute-start | bytes 393224 | tf_op jit(solution)/shard_map/ppermute | solution.py:38

commit v3 on v1

--- a/solution.py
+++ b/solution.py
@@ -34,13 +34,35 @@
     return (owner_dev, local_blk, rank_in, usable)
 
 
+def rows_to_heads_split(x, head_count):
+    rows, cols = x.shape
+    parts = lax.all_to_all(
+        x.reshape(head_count, rows // head_count, cols), "head", split_axis=0, concat_axis=0, tiled=True
+    )
+    return jnp.transpose(parts, (1, 0, 2)).reshape(rows // head_count, head_count * cols)
+
+
+def heads_to_rows_split(y, head_count):
+    rows, cols = y.shape
+    parts = jnp.transpose(y.reshape(rows, head_count, cols // head_count), (1, 0, 2))
+    parts = lax.all_to_all(parts, "head", split_axis=0, concat_axis=0, tiled=True)
+    return parts.reshape(rows * head_count, cols // head_count)
+
+
 def on_device(queries, key_rows, value_rows, out_grad, block_lists):
     pair_count = lax.axis_size("ctx")
+    head_count = lax.axis_size("head")
     half_blocks = QB // 2
     capacity = (QB * (SEL - 1) + pair_count - 2) // (pair_count - 1)
     total_slots = pair_count * capacity
     device = lax.axis_index("ctx")
+    head_idx = lax.axis_index("head")
     score_scale = 1.0 / math.sqrt(HD)
+    rows_here = QB // head_count
+    extras = SEL - 1
+    entry_count = QB * extras
+    my_entries = rows_here * extras
+    part_rows = 2 * BLK // head_count
     owner_dev, local_blk, rank_in, usable = entry_slots(block_lists, half_blocks, pair_count)
     slot_idx = jnp.where(usable, owner_dev * capacity + rank_in, total_slots)
     req_table = (
@@ -49,22 +71,27 @@
     requested = lax.all_to_all(
         req_table.reshape(pair_count, capacity), "ctx", split_axis=0, concat_axis=0, tiled=True
     )
-    head_count = lax.axis_size("head")
-    head_idx = lax.axis_index("head")
-    part_rows = 2 * BLK // head_count
+    q_rows = rows_to_heads_split(queries, head_count)
+    g_rows = rows_to_heads_split(out_grad, head_count)
+    heads_all = q_rows.shape[1] // HD
     kv_blocks = jnp.stack([key_rows.reshape(QB, BLK, HD), value_rows.reshape(QB, BLK, HD)], axis=1)
     kv_parts = kv_blocks.reshape(QB, head_count, part_rows, HD)
     my_part = lax.dynamic_index_in_dim(kv_parts, head_idx, axis=1, keepdims=False)
     send_parts = my_part[jnp.maximum(requested, 0)]
-    fetched_part = lax.all_to_all(send_parts, "ctx", split_axis=0, concat_axis=0, tiled=True)
-    fetched = lax.all_gather(fetched_part, "head", axis=2, tiled=False)
-    kv_table = jnp.concatenate([kv_blocks, fetched.reshape(total_slots, 2, BLK, HD)], axis=0)
-    local_ids = jnp.arange(QB, dtype=jnp.int32)
-    remote_idx = jnp.where(usable, QB + slot_idx, 0).reshape(QB, SEL - 1)
-    entry_idx = jnp.concatenate([local_ids[:, None], remote_idx], axis=1)
-    kv_tiles = kv_table[entry_idx]
+    fetched_part = lax.all_to_all(send_parts, "ctx", split_axis=0, concat_axis=0, tiled=True).reshape(
+        total_slots, part_rows, HD
+    )
+    entry_slot = jnp.where(usable, slot_idx, 0).reshape(head_count, my_entries)
+    share = fetched_part[entry_slot]
+    got = lax.all_to_all(share, "head", split_axis=0, concat_axis=0, tiled=True)
+    remote_kv = jnp.transpose(got, (1, 0, 2, 3)).reshape(rows_here, extras, 2, BLK, HD)
+    first_row = head_idx * rows_here
+    own_kv = lax.dynamic_slice_in_dim(kv_blocks, first_row, rows_here, axis=0)
+    kv_tiles = jnp.concatenate([own_kv[:, None], remote_kv], axis=1)
     key_tile = kv_tiles[:, :, 0]
     value_tile = kv_tiles[:, :, 1]
+    my_lists = lax.dynamic_slice_in_dim(block_lists, first_row, rows_here, axis=0)
+    local_ids = first_row + jnp.arange(rows_here, dtype=jnp.int32)
     own_block = jnp.where(
         local_ids < half_blocks,
         device * half_blocks + local_ids,
@@ -72,13 +99,12 @@
     )
     offsets = jnp.arange(BLK, dtype=jnp.int32)
     query_pos = own_block[:, None] * BLK + offsets[None, :]
-    key_pos = jnp.maximum(block_lists, 0)[:, :, None] * BLK + offsets[None, None, :]
-    visible = (block_lists >= 0)[:, None, :, None] & (
+    key_pos = jnp.maximum(my_lists, 0)[:, :, None] * BLK + offsets[None, None, :]
+    visible = (my_lists >= 0)[:, None, :, None] & (
         key_pos[:, None, :, :] <= query_pos[:, :, None, None]
     )
-    heads_here = queries.shape[1] // HD
-    q_blocks = queries.reshape(QB, BLK, heads_here, HD)
-    g_blocks = out_grad.reshape(QB, BLK, heads_here, HD)
+    q_blocks = q_rows.reshape(rows_here, BLK, heads_all, HD)
+    g_blocks = g_rows.reshape(rows_here, BLK, heads_all, HD)
     scores = (
         jnp.einsum("qihd,qsjd->qhisj", q_blocks, key_tile, preferred_element_type=jnp.float32)
         * score_scale
@@ -120,21 +146,17 @@
         preferred_element_type=jnp.float32,
     )
     grad_tiles = jnp.stack([key_part, value_part], axis=2)
-    entry_count = QB * (SEL - 1)
+    remote_grad = grad_tiles[:, 1:].astype(jnp.bfloat16).reshape(my_entries, head_count, part_rows, HD)
+    back = lax.all_to_all(
+        jnp.transpose(remote_grad, (1, 0, 2, 3)), "head", split_axis=0, concat_axis=0, tiled=True
+    ).reshape(entry_count, part_rows, HD)
     slot_entry = (
         jnp.full((total_slots + 1,), entry_count, jnp.int32)
         .at[slot_idx]
         .set(jnp.arange(entry_count, dtype=jnp.int32))[:total_slots]
     )
-    remote_tiles = jnp.concatenate(
-        [grad_tiles[:, 1:].reshape(entry_count, 2, BLK, HD), jnp.zeros((1, 2, BLK, HD), jnp.float32)],
-        axis=0,
-    )
-    remote_parts = jnp.moveaxis(remote_tiles.reshape(entry_count + 1, head_count, part_rows, HD), 1, 0)
-    outgoing = remote_parts[:, slot_entry].astype(jnp.bfloat16)
-    outgoing_part = lax.psum_scatter(
-        outgoing.reshape(head_count * total_slots * part_rows, HD), "head", scatter_dimension=0, tiled=True
-    )
+    back = jnp.concatenate([back, jnp.zeros((1, part_rows, HD), back.dtype)], axis=0)
+    outgoing_part = back[slot_entry]
     returned = lax.all_to_all(
         outgoing_part.reshape(pair_count, capacity, part_rows, HD),
         "ctx",
@@ -148,20 +170,23 @@
         .at[target]
         .add(returned.reshape(-1, part_rows, HD))[:QB]
     )
-    own_parts = grad_tiles[:, 0].reshape(QB, head_count, part_rows, HD)
-    mine = (jnp.arange(head_count, dtype=jnp.int32) == head_idx)[None, :, None, None]
-    own_parts = own_parts + jnp.where(mine, returned_sum[:, None], 0.0)
-    combined = jnp.transpose(own_parts.reshape(QB, 2, BLK, HD), (1, 0, 2, 3)).reshape(2, QB * BLK, HD)
-    reduced = lax.psum_scatter(
-        combined.astype(jnp.bfloat16), "head", scatter_dimension=1, tiled=True
-    ).astype(jnp.float32)
+    routed = lax.all_to_all(
+        returned_sum.reshape(head_count, rows_here, part_rows, HD),
+        "head",
+        split_axis=0,
+        concat_axis=0,
+        tiled=True,
+    )
+    routed = jnp.transpose(routed, (1, 0, 2, 3)).reshape(rows_here, 2, BLK, HD)
+    final = grad_tiles[:, 0] + routed
+    attended_out = heads_to_rows_split(attended.reshape(rows_here * BLK, heads_all * HD), head_count)
+    query_grad_out = heads_to_rows_split(query_grad.reshape(rows_here * BLK, heads_all * HD), head_count)
     return (
-        attended.reshape(QB * BLK, heads_here * HD),
-        query_grad.reshape(QB * BLK, heads_here * HD),
-        reduced[0].astype(jnp.bfloat16),
-        reduced[1].astype(jnp.bfloat16),
-    )
-
+        attended_out,
+        query_grad_out,
+        final[:, 0].reshape(rows_here * BLK, HD).astype(jnp.bfloat16),
+        final[:, 1].reshape(rows_here * BLK, HD).astype(jnp.bfloat16),
+    )
 
 def solution(mesh):
     return jax.shard_map(

time: 286 us -> 209 us (0.73)
  waiting for transfers between devices: 143 us -> 90.6 us
  starting transfers between devices: 22.8 us -> 41.8 us
  blocking collectives: 34.4 us -> 20.5 us
  between operations: 14.2 us -> 1.07 us
  local copies, waits for them, and re-layouts: 31.7 us -> 22.9 us
  other arithmetic: 21.1 us -> 16.4 us
  matrix products: 18.4 us -> 14.3 us
    reduce_scatter x2 -> x0, waiting for transfers between devices: 63.4 us -> none  [the longest x1 49.9 us: on_device(): lax.psum_scatter(outgoing.reshape(head_count * total_slots * part_rows, H...]
    all_to_all x1 -> x8, waiting for transfers between devices: 7.38 us -> 70.1 us  [the longest x1 28.5 us: on_device(): lax.all_to_all(send_parts, 'ctx', split_axis=0, concat_axis=0, tiled=True)]
    all_gather x1 -> x0, waiting for transfers between devices: 43.8 us -> none  [on_device(): fetched = lax.all_gather(fetched_part, 'head', axis=2, tiled=False)]
    all_to_all x1 -> x8, starting transfers between devices: 12.1 us -> 31.5 us  [the longest x2 7.77 us: rows_to_heads_split(): lax.all_to_all(x.reshape(head_count, rows // head_count, cols), 'head', s...]
    all_to_all x1, blocking collectives: 34.4 us -> 20.5 us  [on_device(): lax.all_to_all(req_table.reshape(pair_count, capacity), 'ctx', split_axis...]
    gather x3 -> x2, local copies, waits for them, and re-layouts: 13 us -> 3.3 us  [the longest x1 1.69 us: on_device(): outgoing_part = back[slot_entry]]
    all_to_all x1, waiting for transfers between devices: 28.5 us -> 20.4 us  [on_device(): lax.all_to_all(outgoing_part.reshape(pair_count, capacity, part_rows, HD)...]
    convert_element_type x2, local copies, waits for them, and re-layouts: 6.98 us -> 1.65 us  [the longest x1 1.34 us: on_device(): query_grad = (jnp.einsum('qhisj,qsjd->qihd', grad_s, key_tile, preferred_...]
  transfers between devices with their start and end apart: 5 -> 9, of which waited for: 5 -> 9; matrix products, arithmetic and copies ran while one was open for 4% -> 15% of each run, Pallas kernels for 0% -> 0%
where the time goes in v3:
time: 209 us; the launch traced here: 208 us
  waiting for transfers between devices  90.6 us (43%)
  starting transfers between devices  41.8 us (20%)
  local copies, waits for them, and re-layouts  22.9 us (11%)
  blocking collectives  20.5 us (10%)
  other arithmetic  16.4 us (8%)
  matrix products  14.3 us (7%)
    all_to_all x1, waiting for transfers between devices, on_device(): lax.all_to_all(send_parts, 'ctx', split_axis=0, concat_axis=0, tiled=True)  28.5 us
    all_to_all x1, blocking collectives, on_device(): lax.all_to_all(req_table.reshape(pair_count, capacity), 'ctx', split_axis...  20.5 us
    all_to_all x1, waiting for transfers between devices, on_device(): lax.all_to_all(outgoing_part.reshape(pair_count, capacity, part_rows, HD)...  20.4 us
    all_to_all x1, starting transfers between devices, on_device(): lax.all_to_all(outgoing_part.reshape(pair_count, capacity, part_rows, HD)...  10.3 us
    all_to_all x1, waiting for transfers between devices, on_device(): lax.all_to_all(jnp.transpose(remote_grad, (1, 0, 2, 3)), 'head', split_ax...  9.12 us
    all_to_all x2, waiting for transfers between devices, rows_to_heads_split(): lax.all_to_all(x.reshape(head_count, rows // head_count, cols), 'head', s...  9.08 us
    all_to_all x1, waiting for transfers between devices, on_device(): got = lax.all_to_all(share, 'head', split_axis=0, concat_axis=0, tiled=True)  8.65 us
    all_to_all x2, waiting for transfers between devices, heads_to_rows_split(): lax.all_to_all(parts, 'head', split_axis=0, concat_axis=0, tiled=True)  8.11 us
  transfers between devices with their start and end apart: 9, of which 9 were waited for; matrix products, arithmetic and copies ran while one was open for 15% of the time, Pallas kernels for 0%

profile of v3, /device:TPU:8, one launch (start us, length us, event | category | flops | bytes accessed | tf_op | source)
XLA Modules:
  0.0 207.6 jit_solution(4323601299524020737)
XLA Ops:
  0.6 0.8 compare_and_fusion.1
  1.4 0.8 fusion.44
  2.3 0.1 ge.47
  2.5 0.1 and.80
  3.0 0.2 select_reduce_fusion
  3.2 0.8 scatter_custom_fusion
  3.9 0.1 copy.81
  4.0 20.5 %all_to_all.57 = s32[64,1,1]{2,1,0:T(1,128)S(1)} all-to-all(s32[64,1,1]{2,1,0:T(1,128)S(1)} %copy.81), channel_id=1, replica_groups=mesh['ctx'=64,'head'=4] {'ctx'}, dimensions={0} | all-to-all | bytes 512 | tf_op jit(solution)/shard_map/all_to_all | solution.py:71
  24.5 4.3 %all-to-all-start.5 = ((bf16[4,256,256]{2,1,0:T(8,128)(2,1)}), bf16[4,256,256]{2,1,0:T(8,128)(2,1)S(1)}, u32[]{:S(2)}, u32[]{:S(2)}) async-start(bf16[4,256,256]{2,1,0:T(8,128)(2,1)} %bitcast.190), calls=%async_computation.5 | async-start | bytes 1048576 | tf_op jit(solution)/shard_map/all_to_all | solution.py:39
  28.8 1.1 pad_maximum_fusion.1
  29.9 2.4 %fusion.65 = (s32[64]{0:T(128)S(1)}, s32[64]{0:T(128)S(1)}) fusion(s32[64,1,1]{2,1,0:T(1,128)S(1)} %all_to_all.57), kind=kLoop, calls=%fused_computation.112 | loop fusion | flops 64 | bytes 768 | tf_op jit(solution)/shard_map/all_to_all | solution.py:71
  32.3 1.7 gather_fusion
  34.0 4.3 %all-to-all-done.5 = bf16[4,256,256]{2,1,0:T(8,128)(2,1)S(1)} async-done(((bf16[4,256,256]{2,1,0:T(8,128)(2,1)}), bf16[4,256,256]{2,1,0:T(8,128)(2,1)S(1)}, u32[]{:S(2)}, u32[]{:S(2)}) %all-to-all-start.5) | async-done | bytes 524320 | tf_op jit(solution)/shard_map/all_to_all | solution.py:39
  38.3 5.5 %all-to-all-start.1 = ((bf16[64,1,64,128]{3,2,1,0:T(8,128)(2,1)}), bf16[64,1,64,128]{3,2,1,0:T(8,128)(2,1)S(1)}, u32[]{:S(2)}, u32[]{:S(2)}) async-start(bf16[64,1,64,128]{3,2,1,0:T(8,128)(2,1)} %bitcast.8), calls=%async_computation.1 | async-start | bytes 2097152 | tf_op jit(solution)/shard_map/all_to_all | solution.py:81
  44.2 28.5 %all-to-all-done.1 = bf16[64,1,64,128]{3,2,1,0:T(8,128)(2,1)S(1)} async-done(((bf16[64,1,64,128]{3,2,1,0:T(8,128)(2,1)}), bf16[64,1,64,128]{3,2,1,0:T(8,128)(2,1)S(1)}, u32[]{:S(2)}, u32[]{:S(2)}) %all-to-all-start.1) | async-done | bytes 1048608 | tf_op jit(solution)/shard_map/all_to_all | solution.py:81
  72.7 3.5 %all-to-all-start.3 = ((bf16[4,256,256]{2,1,0:T(8,128)(2,1)}), bf16[4,256,256]{2,1,0:T(8,128)(2,1)S(1)}, u32[]{:S(2)}, u32[]{:S(2)}) async-start(bf16[4,256,256]{2,1,0:T(8,128)(2,1)} %bitcast.191), calls=%async_computation.3 | async-start | bytes 1048576 | tf_op jit(solution)/shard_map/all_to_all | solution.py:39
  76.2 0.7 fusion.46
  77.0 0.7 maximum_multiply_fusion
  77.7 0.9 copy_bitcast_fusion
  78.6 1.6 gather_fusion.1
  80.2 4.7 %all-to-all-done.3 = bf16[4,256,256]{2,1,0:T(8,128)(2,1)S(1)} async-done(((bf16[4,256,256]{2,1,0:T(8,128)(2,1)}), bf16[4,256,256]{2,1,0:T(8,128)(2,1)S(1)}, u32[]{:S(2)}, u32[]{:S(2)}) %all-to-all-start.3) | async-done | bytes 524320 | tf_op jit(solution)/shard_map/all_to_all | solution.py:39
  85.0 3.7 %all-to-all-start.2 = ((bf16[4,14,64,128]{3,2,1,0:T(8,128)(2,1)}), bf16[4,14,64,128]{3,2,1,0:T(8,128)(2,1)S(1)}, u32[]{:S(2)}, u32[]{:S(2)}) async-start(bf16[4,14,64,128]{3,2,1,0:T(8,128)(2,1)} %bitcast.10), calls=%async_computation.2 | async-start | bytes 1835008 | tf_op jit(solution)/shard_map/all_to_all | solution.py:86
  88.8 0.5 compare_and_fusion
  89.3 0.4 copy.90
  89.7 0.2 reshape_reshape.14
  89.9 1.1 copy.92
  91.0 0.4 copy.84
  91.4 0.2 reshape_reshape.12
  91.6 8.6 %all-to-all-done.2 = bf16[4,14,64,128]{3,2,1,0:T(8,128)(2,1)S(1)} async-done(((bf16[4,14,64,128]{3,2,1,0:T(8,128)(2,1)}), bf16[4,14,64,128]{3,2,1,0:T(8,128)(2,1)S(1)}, u32[]{:S(2)}, u32[]{:S(2)}) %all-to-all-start.2) | async-done | bytes 917536 | tf_op jit(solution)/shard_map/all_to_all | solution.py:86
  100.4 1.3 fusion.5
  101.7 1.8 fusion.2
  103.5 2.9 %multiply_reduce_fusion = (f32[2,128,8]{1,2,0:T(8,128)S(1)}, bf16[2,128,8,128]{1,3,2,0:T(8,128)(2,1)}) fusion(bf16[2,128,8,128]{1,3,2,0:T(8,128)(2,1)S(1)} %copy-done.6, f32[2,128,8]{1,2,0:T(8,128)S(1)} %bitcast.194, f32[2,8,128,128,8]{3,2,4,1,0:T(8,128)S(1)} %get-tuple-element.16, f32[2,8,128]{2,1,0:T(8,128)S(1)} %get-tuple-element.15, ...), kind=kOutput, calls=%fused_computation.36 | convolution fusion | flops 547878912 | bytes 10772480 | tf_op jit(solution)/shard_map/qhisj,qsjd->qihd/dot_general | solution.py:116
  106.5 2.0 fusion.16
  108.5 2.8 %fusion.1 = bf16[2,8,128,8,128]{2,4,1,3,0:T(8,128)(2,1)S(1)} fusion(f32[2,8,128,128,8]{3,2,4,1,0:T(8,128)S(1)} %get-tuple-element.16, f32[2,8,128]{2,1,0:T(8,128)S(1)} %bitcast.195, f32[2,8,128]{2,1,0:T(8,128)S(1)} %log_add_fusion, pred[2,128,8,128]{1,3,2,0:T(8,128)(4,1)S(1)} %compare_and_fusion, bf16[2,128,8,128,1]{3,2,1,0,4:T(8,128)(2,1)S(1)} %bitcast.174, ...), kind=kOutput, calls=%fused_computation.8 | convolution fusion | flops 550502400 | bytes 14434304 | tf_op jit(solution)/shard_map/qihd,qsjd->qhisj/dot_general | solution.py:128
  111.3 1.3 fusion.21
  112.6 0.1 fusion.12
  112.8 0.5 copy-done.2
  113.3 1.0 copy.100
  114.4 3.5 %all-to-all-start.7 = ((bf16[4,14,64,128]{3,2,1,0:T(8,128)(2,1)}), bf16[4,14,64,128]{3,2,1,0:T(8,128)(2,1)S(1)}, u32[]{:S(2)}, u32[]{:S(2)}) async-start(bf16[4,14,64,128]{3,2,1,0:T(8,128)(2,1)} %copy.100), calls=%async_computation.7 | async-start | bytes 1835008 | tf_op jit(solution)/shard_map/all_to_all | solution.py:150
  117.9 0.3 copy.88
  118.2 0.3 reshape_reshape.13
  118.5 0.9 copy.89
  119.4 9.1 %all-to-all-done.7 = bf16[4,14,64,128]{3,2,1,0:T(8,128)(2,1)S(1)} async-done(((bf16[4,14,64,128]{3,2,1,0:T(8,128)(2,1)}), bf16[4,14,64,128]{3,2,1,0:T(8,128)(2,1)S(1)}, u32[]{:S(2)}, u32[]{:S(2)}) %all-to-all-start.7) | async-done | bytes 917536 | tf_op jit(solution)/shard_map/all_to_all | solution.py:150
  128.5 3.5 %all-to-all-start.4 = ((bf16[4,256,256]{2,1,0:T(8,128)(2,1)}), bf16[4,256,256]{2,1,0:T(8,128)(2,1)S(1)}, u32[]{:S(2)}, u32[]{:S(2)}) async-start(bf16[4,256,256]{2,1,0:T(8,128)(2,1)} %copy.89), calls=%async_computation.4 | async-start | bytes 1048576 | tf_op jit(solution)/shard_map/all_to_all | solution.py:48
  132.0 1.0 scatter_custom_fusion.1
  133.1 1.7 gather_fusion.2
  134.8 5.3 %all-to-all-done.4 = bf16[4,256,256]{2,1,0:T(8,128)(2,1)S(1)} async-done(((bf16[4,256,256]{2,1,0:T(8,128)(2,1)}), bf16[4,256,256]{2,1,0:T(8,128)(2,1)S(1)}, u32[]{:S(2)}, u32[]{:S(2)}) %all-to-all-start.4) | async-done | bytes 524320 | tf_op jit(solution)/shard_map/all_to_all | solution.py:48
  140.1 10.3 %all-to-all-start.8 = ((bf16[64,1,64,128]{3,2,1,0:T(8,128)(2,1)}), bf16[64,1,64,128]{3,2,1,0:T(8,128)(2,1)S(1)}, u32[]{:S(2)}, u32[]{:S(2)}) async-start(bf16[64,1,64,128]{3,2,1,0:T(8,128)(2,1)} %bitcast.55), calls=%async_computation.8 | async-start | bytes 2097152 | tf_op jit(solution)/shard_map/all_to_all | solution.py:160
  150.4 3.9 %fusion.23 = bf16[2,128,8,128]{1,3,2,0:T(8,128)(2,1)} fusion(bf16[2,8,128,8,128]{2,4,1,3,0:T(8,128)(2,1)} %copy-done.2, bf16[2,1,2,128,128]{4,3,1,0,2:T(8,128)(2,1)} %copy-done.7, bf16[2,7,2,128,128]{4,3,2,1,0:T(8,128)(2,1)} %bitcast.188), kind=kOutput, calls=%fused_computation.32 | convolution fusion | flops 538443776 | bytes 5767168 | tf_op jit(solution)/shard_map/qhisj,qsjd->qihd/dot_general | solution.py:135
  154.3 1.3 copy.95
  155.7 1.1 reshape_reshape.15
  156.8 1.9 copy.96
  158.7 20.4 %all-to-all-done.8 = bf16[64,1,64,128]{3,2,1,0:T(8,128)(2,1)S(1)} async-done(((bf16[64,1,64,128]{3,2,1,0:T(8,128)(2,1)}), bf16[64,1,64,128]{3,2,1,0:T(8,128)(2,1)S(1)}, u32[]{:S(2)}, u32[]{:S(2)}) %all-to-all-start.8) | async-done | bytes 1048608 | tf_op jit(solution)/shard_map/all_to_all | solution.py:160
  179.1 4.1 %all-to-all-start.6 = ((bf16[4,256,256]{2,1,0:T(8,128)(2,1)}), bf16[4,256,256]{2,1,0:T(8,128)(2,1)}, u32[]{:S(2)}, u32[]{:S(2)}) async-start(bf16[4,256,256]{2,1,0:T(8,128)(2,1)} %copy.96), calls=%async_computation.6 | async-start | bytes 1048576 | tf_op jit(solution)/shard_map/all_to_all | solution.py:48
  183.3 1.5 bitcast_convert_fusion
  184.8 3.8 %scatter_fusion = f32[9,64,128]{2,1,0:T(8,128)S(1)} fusion(f32[9,64,128]{2,1,0:T(8,128)S(1)} %broadcast_in_dim.34, s32[64]{0:T(128)S(1)} %fusion.52, f32[64,64,128]{2,1,0:T(8,128)S(1)} %bitcast_convert_fusion), kind=kCustom, calls=%fused_computation.5 | custom fusion | flops 524288 | bytes 6291712 | tf_op jit(solution)/shard_map/scatter-add | solution.py:171
  188.6 0.7 slice.53
  189.3 2.8 %all-to-all-done.6 = bf16[4,256,256]{2,1,0:T(8,128)(2,1)} async-done(((bf16[4,256,256]{2,1,0:T(8,128)(2,1)}), bf16[4,256,256]{2,1,0:T(8,128)(2,1)}, u32[]{:S(2)}, u32[]{:S(2)}) %all-to-all-start.6) | async-done | bytes 524320 | tf_op jit(solution)/shard_map/all_to_all | solution.py:48
  192.1 3.4 %all-to-all-start.9 = ((f32[4,2,64,128]{3,2,1,0:T(8,128)}), f32[4,2,64,128]{3,2,1,0:T(8,128)S(1)}, u32[]{:S(2)}, u32[]{:S(2)}) async-start(f32[4,2,64,128]{3,2,1,0:T(8,128)} %bitcast.58), calls=%async_computation.9 | async-start | bytes 524288 | tf_op jit(solution)/shard_map/all_to_all | solution.py:173
  195.5 6.6 %all-to-all-done.9 = f32[4,2,64,128]{3,2,1,0:T(8,128)S(1)} async-done(((f32[4,2,64,128]{3,2,1,0:T(8,128)}), f32[4,2,64,128]{3,2,1,0:T(8,128)S(1)}, u32[]{:S(2)}, u32[]{:S(2)}) %all-to-all-start.9) | async-done | bytes 262176 | tf_op jit(solution)/shard_map/all_to_all | solution.py:173
  202.2 1.0 fusion.37
  203.2 0.7 fusion.66
  203.8 1.9 copy.160
  205.7 1.9 copy.161
  (49 shorter events, 1.5 us)
Async XLA Ops:
  24.5 13.8 %all-to-all-start.5 = ((bf16[4,256,256]{2,1,0:T(8,128)(2,1)}), bf16[4,256,256]{2,1,0:T(8,128)(2,1)S(1)}, u32[]{:S(2)}, u32[]{:S(2)}) async-start(bf16[4,256,256]{2,1,0:T(8,128)(2,1)} %bitcast.190), calls=%async_computation.5 | async-start | bytes 1048576 | tf_op jit(solution)/shard_map/all_to_all | solution.py:39
  38.3 34.4 %all-to-all-start.1 = ((bf16[64,1,64,128]{3,2,1,0:T(8,128)(2,1)}), bf16[64,1,64,128]{3,2,1,0:T(8,128)(2,1)S(1)}, u32[]{:S(2)}, u32[]{:S(2)}) async-start(bf16[64,1,64,128]{3,2,1,0:T(8,128)(2,1)} %bitcast.8), calls=%async_computation.1 | async-start | bytes 2097152 | tf_op jit(solution)/shard_map/all_to_all | solution.py:81
  72.7 12.2 %all-to-all-start.3 = ((bf16[4,256,256]{2,1,0:T(8,128)(2,1)}), bf16[4,256,256]{2,1,0:T(8,128)(2,1)S(1)}, u32[]{:S(2)}, u32[]{:S(2)}) async-start(bf16[4,256,256]{2,1,0:T(8,128)(2,1)} %bitcast.191), calls=%async_computation.3 | async-start | bytes 1048576 | tf_op jit(solution)/shard_map/all_to_all | solution.py:39
  78.6 29.9 %copy-start.7 = (bf16[2,1,2,128,128]{4,3,1,0,2:T(8,128)(2,1)}, bf16[2,1,2,128,128]{4,3,1,0,2:T(8,128)(2,1)S(1)}, u32[]{:S(2)}) copy-start(bf16[2,1,2,128,128]{4,3,1,0,2:T(8,128)(2,1)S(1)} %copy_bitcast_fusion) | copy-start | bytes 393220
  85.0 15.3 %all-to-all-start.2 = ((bf16[4,14,64,128]{3,2,1,0:T(8,128)(2,1)}), bf16[4,14,64,128]{3,2,1,0:T(8,128)(2,1)S(1)}, u32[]{:S(2)}, u32[]{:S(2)}) async-start(bf16[4,14,64,128]{3,2,1,0:T(8,128)(2,1)} %bitcast.10), calls=%async_computation.2 | async-start | bytes 1835008 | tf_op jit(solution)/shard_map/all_to_all | solution.py:86
  100.4 8.1 %copy-start.4 = (bf16[14,4,64,128]{3,2,1,0:T(8,128)(2,1)}, bf16[14,4,64,128]{3,2,1,0:T(8,128)(2,1)S(1)}, u32[]{:S(2)}) copy-start(bf16[14,4,64,128]{3,2,1,0:T(8,128)(2,1)S(1)} %copy.82) | copy-start | bytes 2752516
  100.4 3.1 %copy-start.6 = (bf16[2,128,8,128]{1,3,2,0:T(8,128)(2,1)S(1)}, bf16[2,128,8,128]{1,3,2,0:T(8,128)(2,1)}, u32[]{:S(2)}) copy-start(bf16[2,128,8,128]{1,3,2,0:T(8,128)(2,1)} %copy.92) | copy-start | bytes 1572868
  108.5 4.1 %copy-start = (f32[2,8,1,128,128]{4,3,1,0,2:T(8,128)}, f32[2,8,1,128,128]{4,3,1,0,2:T(8,128)S(1)}, u32[]{:S(2)}) copy-start(f32[2,8,1,128,128]{4,3,1,0,2:T(8,128)S(1)} %fusion.16) | copy-start | bytes 3145732
  111.3 1.9 copy-start.2
  111.3 6.5 %copy-start.5 = (bf16[2,128,8,128]{1,3,2,0:T(8,128)(2,1)S(1)}, bf16[2,128,8,128]{1,3,2,0:T(8,128)(2,1)}, u32[]{:S(2)}) copy-start(bf16[2,128,8,128]{1,3,2,0:T(8,128)(2,1)} %get-tuple-element.18) | copy-start | bytes 1572868
  114.4 14.2 %all-to-all-start.7 = ((bf16[4,14,64,128]{3,2,1,0:T(8,128)(2,1)}), bf16[4,14,64,128]{3,2,1,0:T(8,128)(2,1)S(1)}, u32[]{:S(2)}, u32[]{:S(2)}) async-start(bf16[4,14,64,128]{3,2,1,0:T(8,128)(2,1)} %copy.100), calls=%async_computation.7 | async-start | bytes 1835008 | tf_op jit(solution)/shard_map/all_to_all | solution.py:150
  128.5 11.5 %all-to-all-start.4 = ((bf16[4,256,256]{2,1,0:T(8,128)(2,1)}), bf16[4,256,256]{2,1,0:T(8,128)(2,1)S(1)}, u32[]{:S(2)}, u32[]{:S(2)}) async-start(bf16[4,256,256]{2,1,0:T(8,128)(2,1)} %copy.89), calls=%async_computation.4 | async-start | bytes 1048576 | tf_op jit(solution)/shard_map/all_to_all | solution.py:48
  140.1 43.2 %copy-start.3 = (bf16[4,256,256]{2,1,0:T(8,128)(2,1)}, bf16[4,256,256]{2,1,0:T(8,128)(2,1)S(1)}, u32[]{:S(2)}) copy-start(bf16[4,256,256]{2,1,0:T(8,128)(2,1)S(1)} %all-to-all-done.4) | copy-start | bytes 1572868
  140.1 39.1 %all-to-all-start.8 = ((bf16[64,1,64,128]{3,2,1,0:T(8,128)(2,1)}), bf16[64,1,64,128]{3,2,1,0:T(8,128)(2,1)S(1)}, u32[]{:S(2)}, u32[]{:S(2)}) async-start(bf16[64,1,64,128]{3,2,1,0:T(8,128)(2,1)} %bitcast.55), calls=%async_computation.8 | async-start | bytes 2097152 | tf_op jit(solution)/shard_map/all_to_all | solution.py:160
  179.1 4.2 %copy-start.1 = (bf16[64,1,64,128]{3,2,1,0:T(8,128)(2,1)}, bf16[64,1,64,128]{3,2,1,0:T(8,128)(2,1)S(1)}, u32[]{:S(2)}) copy-start(bf16[64,1,64,128]{3,2,1,0:T(8,128)(2,1)S(1)} %all-to-all-done.8) | copy-start | bytes 3145732
  179.1 13.0 %all-to-all-start.6 = ((bf16[4,256,256]{2,1,0:T(8,128)(2,1)}), bf16[4,256,256]{2,1,0:T(8,128)(2,1)}, u32[]{:S(2)}, u32[]{:S(2)}) async-start(bf16[4,256,256]{2,1,0:T(8,128)(2,1)} %copy.96), calls=%async_computation.6 | async-start | bytes 1048576 | tf_op jit(solution)/shard_map/all_to_all | solution.py:48
  192.1 10.1 %all-to-all-start.9 = ((f32[4,2,64,128]{3,2,1,0:T(8,128)}), f32[4,2,64,128]{3,2,1,0:T(8,128)S(1)}, u32[]{:S(2)}, u32[]{:S(2)}) async-start(f32[4,2,64,128]{3,2,1,0:T(8,128)} %bitcast.58), calls=%async_computation.9 | async-start | bytes 524288 | tf_op jit(solution)/shard_map/all_to_all | solution.py:173

commit v4 on v3

--- a/solution.py
+++ b/solution.py
@@ -34,18 +34,25 @@
     return (owner_dev, local_blk, rank_in, usable)
 
 
+def head_exchange(x, head_idx, count):
+    got = [lax.dynamic_index_in_dim(x, head_idx, axis=0, keepdims=False)]
+    for k in range(1, count):
+        piece = lax.dynamic_index_in_dim(x, (head_idx + k) % count, axis=0, keepdims=False)
+        got.append(lax.ppermute(piece, "head", [(j, (j + k) % count) for j in range(count)]))
+    order = (head_idx - jnp.arange(count, dtype=jnp.int32)) % count
+    return jnp.stack(got)[order]
+
+
 def rows_to_heads_split(x, head_count):
     rows, cols = x.shape
-    parts = lax.all_to_all(
-        x.reshape(head_count, rows // head_count, cols), "head", split_axis=0, concat_axis=0, tiled=True
-    )
+    parts = head_exchange(x.reshape(head_count, rows // head_count, cols), lax.axis_index("head"), head_count)
     return jnp.transpose(parts, (1, 0, 2)).reshape(rows // head_count, head_count * cols)
 
 
 def heads_to_rows_split(y, head_count):
     rows, cols = y.shape
     parts = jnp.transpose(y.reshape(rows, head_count, cols // head_count), (1, 0, 2))
-    parts = lax.all_to_all(parts, "head", split_axis=0, concat_axis=0, tiled=True)
+    parts = head_exchange(parts, lax.axis_index("head"), head_count)
     return parts.reshape(rows * head_count, cols // head_count)
 
 

time: 209 us -> 173 us (0.83)
  waiting for transfers between devices: 90.6 us -> 50.4 us
  blocking collectives: 20.5 us -> 0 us
  starting transfers between devices: 41.8 us -> 57.2 us
  local copies, waits for them, and re-layouts: 22.9 us -> 29.6 us
  other arithmetic: 16.4 us -> 20.9 us
    all_to_all x1 -> x0, blocking collectives: 20.5 us -> none  [on_device(): lax.all_to_all(req_table.reshape(pair_count, capacity), 'ctx', split_axis...]
    ppermute x0 -> x12, starting transfers between devices: none -> 19.6 us  [head_exchange(): lax.ppermute(piece, 'head', [(j, (j + k) % count) for j in range(count)])]
    all_to_all x1, waiting for transfers between devices: 20.4 us -> 7.83 us  [on_device(): lax.all_to_all(outgoing_part.reshape(pair_count, capacity, part_rows, HD)...]
    all_to_all x1, waiting for transfers between devices: 28.5 us -> 16.7 us  [on_device(): lax.all_to_all(send_parts, 'ctx', split_axis=0, concat_axis=0, tiled=True)]
    all_to_all x4 -> x1, waiting for transfers between devices: 17.2 us -> 7.43 us  [on_device(): lax.all_to_all(req_table.reshape(pair_count, capacity), 'ctx', split_axis...]
    all_to_all x1, waiting for transfers between devices: 8.65 us -> 0.01 us  [on_device(): got = lax.all_to_all(share, 'head', split_axis=0, concat_axis=0, tiled=True)]
    ppermute x0 -> x12, waiting for transfers between devices: none -> 7.24 us  [head_exchange(): lax.ppermute(piece, 'head', [(j, (j + k) % count) for j in range(count)])]
    all_to_all x1, waiting for transfers between devices: 6.64 us -> 1.28 us  [on_device(): lax.all_to_all(returned_sum.reshape(head_count, rows_here, part_rows, HD)...]
  transfers between devices with their start and end apart: 9 -> 18, of which waited for: 9 -> 6; matrix products, arithmetic and copies ran while one was open for 15% -> 21% of each run, Pallas kernels for 0% -> 0%
where the time goes in v4:
time: 173 us; the launch traced here: 172 us
  starting transfers between devices  57.2 us (33%)
  waiting for transfers between devices  50.4 us (29%)
  local copies, waits for them, and re-layouts  29.6 us (17%)
  other arithmetic  20.9 us (12%)
  matrix products  12.8 us (7%)
    ppermute x12, starting transfers between devices, head_exchange(): lax.ppermute(piece, 'head', [(j, (j + k) % count) for j in range(count)])  19.6 us
    all_to_all x1, waiting for transfers between devices, on_device(): lax.all_to_all(send_parts, 'ctx', split_axis=0, concat_axis=0, tiled=True)  16.7 us
    all_to_all x1, starting transfers between devices, on_device(): lax.all_to_all(req_table.reshape(pair_count, capacity), 'ctx', split_axis...  12.1 us
    all_to_all x1, waiting for transfers between devices, on_device(): lax.all_to_all(jnp.transpose(remote_grad, (1, 0, 2, 3)), 'head', split_ax...  9.92 us
    all_to_all x1, starting transfers between devices, on_device(): lax.all_to_all(outgoing_part.reshape(pair_count, capacity, part_rows, HD)...  8.36 us
    all_to_all x1, waiting for transfers between devices, on_device(): lax.all_to_all(outgoing_part.reshape(pair_count, capacity, part_rows, HD)...  7.83 us
    all_to_all x1, waiting for transfers between devices, on_device(): lax.all_to_all(req_table.reshape(pair_count, capacity), 'ctx', split_axis...  7.43 us
    ppermute x12, waiting for transfers between devices, head_exchange(): lax.ppermute(piece, 'head', [(j, (j + k) % count) for j in range(count)])  7.24 us
  transfers between devices with their start and end apart: 18, of which 6 were waited for; matrix products, arithmetic and copies ran while one was open for 21% of the time, Pallas kernels for 0%

profile of v4, /device:TPU:8, one launch (start us, length us, event | category | flops | bytes accessed | tf_op | source)
XLA Modules:
  0.0 172.1 jit_solution(12097871113440831274)
XLA Ops:
  0.7 0.8 fusion.44
  1.5 0.8 compare_and_fusion.1
  3.2 0.7 scatter_custom_fusion
  4.0 0.7 copy.75
  4.7 12.1 %all-to-all-start = ((s32[64,1,1]{2,1,0:T(1,128)}), s32[64,1,1]{2,1,0:T(1,128)S(1)}, u32[]{:S(2)}, u32[]{:S(2)}) async-start(s32[64,1,1]{2,1,0:T(1,128)} %copy.75), calls=%async_computation | async-start | bytes 65536 | tf_op jit(solution)/shard_map/all_to_all | solution.py:78
  16.8 1.1 pad_maximum_fusion.1
  17.9 7.4 %all-to-all-done = s32[64,1,1]{2,1,0:T(1,128)S(1)} async-done(((s32[64,1,1]{2,1,0:T(1,128)}), s32[64,1,1]{2,1,0:T(1,128)S(1)}, u32[]{:S(2)}, u32[]{:S(2)}) %all-to-all-start) | async-done | bytes 288 | tf_op jit(solution)/shard_map/all_to_all | solution.py:78
  25.4 2.8 %fusion.67 = (s32[64]{0:T(128)}, s32[64]{0:T(128)S(1)}) fusion(s32[64,1,1]{2,1,0:T(1,128)S(1)} %all-to-all-done), kind=kLoop, calls=%fused_computation.151 | loop fusion | flops 64 | bytes 768 | tf_op jit(solution)/shard_map/all_to_all | solution.py:78
  28.2 1.7 gather_fusion
  29.8 5.5 %all-to-all-start.1 = ((bf16[64,1,64,128]{3,2,1,0:T(8,128)(2,1)}), bf16[64,1,64,128]{3,2,1,0:T(8,128)(2,1)S(1)}, u32[]{:S(2)}, u32[]{:S(2)}) async-start(bf16[64,1,64,128]{3,2,1,0:T(8,128)(2,1)} %bitcast.8), calls=%async_computation.1 | async-start | bytes 2097152 | tf_op jit(solution)/shard_map/all_to_all | solution.py:88
  35.4 1.1 constant_dynamic-slice_fusion.9
  36.6 1.6 collective-permute-start
  38.1 2.7 %collective-permute-start.1 = (bf16[256,256]{1,0:T(8,128)(2,1)S(1)}, bf16[256,256]{1,0:T(8,128)(2,1)S(1)}, u32[]{:S(2)}, u32[]{:S(2)}) collective-permute-start(bf16[256,256]{1,0:T(8,128)(2,1)S(1)} %get-tuple-element.24), channel_id=1, source_target_pairs={{0,2},{1,3},{2,0},{3,1},{4,6},{5,7},{6,4},{7,5},{8,10},{9,11},{10,... | collective-permute-start | bytes 393224 | tf_op jit(solution)/shard_map/ppermute | solution.py:41
  40.9 1.4 collective-permute-start.2
  42.3 1.8 %constant_dynamic-slice_fusion.4 = (bf16[1,256,256]{2,1,0:T(8,128)(2,1)S(1)}, bf16[256,256]{1,0:T(8,128)(2,1)S(1)}, bf16[256,256]{1,0:T(8,128)(2,1)S(1)}, bf16[256,256]{1,0:T(8,128)(2,1)}) fusion(bf16[4,256,256]{2,1,0:T(8,128)(2,1)} %bitcast.236, s32[]{:T(128)S(6)} %select_n.252, s32[]{:T(128)S(6)} %select_n.272, s32[]{:T(128)S(6)} %select_n.270, ...), kind=kLoop, calls=%fused_computation.93 | loop fusion | bytes 1048592 | tf_op jit(solution)/shard_map/jit(dynamic_index_in_dim)/dynamic_slice | solution.py:38
  44.7 0.9 collective-permute-start.7
  46.0 0.7 fusion.46
  46.7 0.7 maximum_multiply_fusion
  47.5 16.7 %all-to-all-done.1 = bf16[64,1,64,128]{3,2,1,0:T(8,128)(2,1)S(1)} async-done(((bf16[64,1,64,128]{3,2,1,0:T(8,128)(2,1)}), bf16[64,1,64,128]{3,2,1,0:T(8,128)(2,1)S(1)}, u32[]{:S(2)}, u32[]{:S(2)}) %all-to-all-start.1) | async-done | bytes 1048608 | tf_op jit(solution)/shard_map/all_to_all | solution.py:88
  64.2 1.6 gather_fusion.1
  65.8 4.3 %all-to-all-start.2 = ((bf16[4,14,64,128]{3,2,1,0:T(8,128)(2,1)}), bf16[4,14,64,128]{3,2,1,0:T(8,128)(2,1)S(1)}, u32[]{:S(2)}, u32[]{:S(2)}) async-start(bf16[4,14,64,128]{3,2,1,0:T(8,128)(2,1)} %bitcast.10), calls=%async_computation.2 | async-start | bytes 1835008 | tf_op jit(solution)/shard_map/all_to_all | solution.py:93
  70.7 3.5 %collective-permute-start.8 = (bf16[256,256]{1,0:T(8,128)(2,1)S(1)}, bf16[256,256]{1,0:T(8,128)(2,1)}, u32[]{:S(2)}, u32[]{:S(2)}) collective-permute-start(bf16[256,256]{1,0:T(8,128)(2,1)S(1)} %get-tuple-element.15), channel_id=1, source_target_pairs={{0,3},{1,0},{2,1},{3,2},{4,7},{5,4},{6,5},{7,6},{8,11},{9,8},{10,9... | collective-permute-start | bytes 393224 | tf_op jit(solution)/shard_map/ppermute | solution.py:41
  74.2 0.6 copy-done.5
  74.9 1.0 pad_maximum_fusion.3
  77.1 7.2 %collective-permute-done.8 = bf16[256,256]{1,0:T(8,128)(2,1)} collective-permute-done((bf16[256,256]{1,0:T(8,128)(2,1)S(1)}, bf16[256,256]{1,0:T(8,128)(2,1)}, u32[]{:S(2)}, u32[]{:S(2)}) %collective-permute-start.8) | collective-permute-done | bytes 131104 | tf_op jit(solution)/shard_map/ppermute | solution.py:41
  84.3 1.0 pad_maximum_fusion.5
  86.9 1.3 fusion.5
  88.3 1.8 %fusion.2 = f32[2,8,128]{2,1,0:T(8,128)S(1)} fusion(f32[2,8,128,128,8]{3,2,4,1,0:T(8,128)S(1)} %get-tuple-element.32, f32[2,8,128]{2,1,0:T(8,128)S(1)} %get-tuple-element.31, pred[2,128,8,128]{1,3,2,0:T(8,128)(4,1)S(1)} %compare_and_fusion), kind=kLoop, calls=%fused_computation.16 | loop fusion | flops 8386560 | bytes 8667136 | tf_op jit(solution)/shard_map/reduce_sum | solution.py:122
  90.1 2.0 %fusion.16 = f32[2,8,1,128,128]{4,3,1,0,2:T(8,128)S(1)} fusion(f32[2,8,128,128,8]{3,2,4,1,0:T(8,128)S(1)} %get-tuple-element.32, f32[2,8,128]{2,1,0:T(8,128)S(1)} %log_add_fusion, pred[2,128,8,128]{1,3,2,0:T(8,128)(4,1)S(1)} %compare_and_fusion, bf16[2,128,8,128,1]{3,2,1,0,4:T(8,128)(2,1)S(1)} %bitcast.218), kind=kOutput, calls=%fused_computation.29 | convolution fusion | flops 545259520 | bytes 10231808 | tf_op jit(solution)/shard_map/qhisj,qihd->qsjd/dot_general | solution.py:149
  92.1 2.3 %multiply_reduce_fusion = (f32[2,128,8]{1,2,0:T(8,128)S(1)}, bf16[2,128,8,128]{1,3,2,0:T(8,128)(2,1)S(1)}) fusion(bf16[2,128,8,128]{1,3,2,0:T(8,128)(2,1)S(1)} %copy.85, f32[2,128,8]{1,2,0:T(8,128)S(1)} %bitcast.250, f32[2,8,128,128,8]{3,2,4,1,0:T(8,128)S(1)} %get-tuple-element.32, f32[2,8,128]{2,1,0:T(8,128)S(1)} %get-tuple-element.31, ...), kind=kOutput, calls=%fused_computation.40 | convolution fusion | flops 547878912 | bytes 10772480 | tf_op jit(solution)/shard_map/qhisj,qsjd->qihd/dot_general | solution.py:123
  94.4 2.8 %fusion.1 = bf16[2,8,128,8,128]{2,4,1,3,0:T(8,128)(2,1)S(1)} fusion(f32[2,8,128,128,8]{3,2,4,1,0:T(8,128)S(1)} %get-tuple-element.32, f32[2,8,128]{2,1,0:T(8,128)S(1)} %bitcast.251, f32[2,8,128]{2,1,0:T(8,128)S(1)} %log_add_fusion, pred[2,128,8,128]{1,3,2,0:T(8,128)(4,1)S(1)} %compare_and_fusion, bf16[2,128,8,128,1]{3,2,1,0,4:T(8,128)(2,1)S(1)} %bitcast.219, ...), kind=kOutput, calls=%fused_computation.12 | convolution fusion | flops 550502400 | bytes 14434304 | tf_op jit(solution)/shard_map/qihd,qsjd->qhisj/dot_general | solution.py:135
  97.2 1.2 fusion.21
  99.3 1.0 copy.92
  100.3 3.9 %all-to-all-start.3 = ((bf16[4,14,64,128]{3,2,1,0:T(8,128)(2,1)}), bf16[4,14,64,128]{3,2,1,0:T(8,128)(2,1)S(1)}, u32[]{:S(2)}, u32[]{:S(2)}) async-start(bf16[4,14,64,128]{3,2,1,0:T(8,128)(2,1)} %copy.92), calls=%async_computation.3 | async-start | bytes 1835008 | tf_op jit(solution)/shard_map/all_to_all | solution.py:157
  104.2 0.7 scatter_custom_fusion.1
  105.6 9.9 %all-to-all-done.3 = bf16[4,14,64,128]{3,2,1,0:T(8,128)(2,1)S(1)} async-done(((bf16[4,14,64,128]{3,2,1,0:T(8,128)(2,1)}), bf16[4,14,64,128]{3,2,1,0:T(8,128)(2,1)S(1)}, u32[]{:S(2)}, u32[]{:S(2)}) %all-to-all-start.3) | async-done | bytes 917536 | tf_op jit(solution)/shard_map/all_to_all | solution.py:157
  115.6 1.8 %gather_fusion.6 = bf16[64,64,128]{2,1,0:T(8,128)(2,1)} fusion(bf16[57,64,128]{2,1,0:T(8,128)(2,1)S(1)} %concatenate.7, s32[1024]{0:T(1024)} %pad_clamp_fusion), kind=kCustom, calls=%fused_computation.6 | custom fusion | bytes 2097408 | tf_op jit(solution)/shard_map/gather | solution.py:166
  117.4 8.4 %all-to-all-start.4 = ((bf16[64,1,64,128]{3,2,1,0:T(8,128)(2,1)}), bf16[64,1,64,128]{3,2,1,0:T(8,128)(2,1)}, u32[]{:S(2)}, u32[]{:S(2)}) async-start(bf16[64,1,64,128]{3,2,1,0:T(8,128)(2,1)} %bitcast.72), calls=%async_computation.4 | async-start | bytes 2097152 | tf_op jit(solution)/shard_map/all_to_all | solution.py:167
  125.8 3.1 %fusion.23 = bf16[2,128,8,128]{1,3,2,0:T(8,128)(2,1)S(1)} fusion(bf16[2,8,128,8,128]{2,4,1,3,0:T(8,128)(2,1)} %copy-done.1, bf16[2,1,2,128,128]{4,3,1,0,2:T(8,128)(2,1)S(1)} %copy_bitcast_fusion.8, bf16[2,7,2,128,128]{4,3,2,1,0:T(8,128)(2,1)} %bitcast.233), kind=kOutput, calls=%fused_computation.36 | convolution fusion | flops 538443776 | bytes 5767168 | tf_op jit(solution)/shard_map/qhisj,qsjd->qihd/dot_general | solution.py:142
  130.2 2.2 %constant_dynamic-slice_fusion.3 = (bf16[256,1,256]{2,1,0:T(2,128)(2,1)S(1)}, bf16[256,1,256]{2,1,0:T(2,128)(2,1)S(1)}, bf16[256,1,256]{2,1,0:T(2,128)(2,1)S(1)}...) fusion(bf16[256,4,256]{2,1,0:T(4,128)(2,1)S(1)} %reshape_reshap, ...), kind=kLoop, calls=%fused_computation.92 | loop fusion | bytes 2097168 | tf_op jit(solution)/shard_map/dynamic-slice.4
  132.4 0.6 collective-permute-start.9
  133.1 0.7 copy.166
  133.7 2.1 %collective-permute-start.10 = (bf16[256,256]{1,0:T(8,128)(2,1)}, bf16[256,256]{1,0:T(8,128)(2,1)}, u32[]{:S(2)}, u32[]{:S(2)}) collective-permute-start(bf16[256,256]{1,0:T(8,128)(2,1)} %bitcast.205), channel_id=1, source_target_pairs={{0,2},{1,3},{2,0},{3,1},{4,6},{5,7},{6,4},{7,5},{8,10},{9,11},{10,... | collective-permute-start | bytes 393224 | tf_op jit(solution)/shard_map/ppermute | solution.py:41
  135.8 0.7 copy.165
  137.1 0.7 copy.168
  137.8 0.7 copy.171
  138.4 1.4 collective-permute-start.3
  139.8 0.7 copy.170
  140.5 1.5 collective-permute-start.4
  142.0 0.7 copy.169
  142.7 0.7 copy.172
  144.0 2.6 %collective-permute-start.5 = (bf16[256,256]{1,0:T(8,128)(2,1)}, bf16[256,256]{1,0:T(8,128)(2,1)}, u32[]{:S(2)}, u32[]{:S(2)}) collective-permute-start(bf16[256,256]{1,0:T(8,128)(2,1)} %bitcast.208), channel_id=1, source_target_pairs={{0,3},{1,0},{2,1},{3,2},{4,7},{5,4},{6,5},{7,6},{8,11},{9,8},{10,9... | collective-permute-start | bytes 393224 | tf_op jit(solution)/shard_map/ppermute | solution.py:41
  146.6 7.8 %all-to-all-done.4 = bf16[64,1,64,128]{3,2,1,0:T(8,128)(2,1)} async-done(((bf16[64,1,64,128]{3,2,1,0:T(8,128)(2,1)}), bf16[64,1,64,128]{3,2,1,0:T(8,128)(2,1)}, u32[]{:S(2)}, u32[]{:S(2)}) %all-to-all-start.4) | async-done | bytes 1048608 | tf_op jit(solution)/shard_map/all_to_all | solution.py:167
  154.5 1.5 bitcast_convert_fusion
  156.0 3.8 %scatter_fusion = f32[9,64,128]{2,1,0:T(8,128)S(1)} fusion(f32[9,64,128]{2,1,0:T(8,128)S(1)} %broadcast_in_dim.30, s32[64]{0:T(128)S(1)} %fusion.54, f32[64,64,128]{2,1,0:T(8,128)S(1)} %bitcast_convert_fusion), kind=kCustom, calls=%fused_computation.9 | custom fusion | flops 524288 | bytes 6291712 | tf_op jit(solution)/shard_map/scatter-add | solution.py:178
  159.7 0.7 slice.61
  160.4 3.4 %all-to-all-start.5 = ((f32[4,2,64,128]{3,2,1,0:T(8,128)}), f32[4,2,64,128]{3,2,1,0:T(8,128)S(1)}, u32[]{:S(2)}, u32[]{:S(2)}) async-start(f32[4,2,64,128]{3,2,1,0:T(8,128)} %bitcast.75), calls=%async_computation.5 | async-start | bytes 524288 | tf_op jit(solution)/shard_map/all_to_all | solution.py:180
  163.9 1.2 pad_maximum_fusion.6
  165.0 1.5 gather_fusion.5
  166.5 1.2 pad_maximum_fusion.4
  167.7 1.5 gather_fusion.3
  169.2 1.3 all-to-all-done.5
  170.5 1.0 fusion.37
  171.5 0.7 fusion.68
  (85 shorter events, 9.6 us)
Async XLA Ops:
  0.6 70.0 %copy-start.2 = (bf16[1024,128]{1,0:T(8,128)(2,1)S(1)}, bf16[1024,128]{1,0:T(8,128)(2,1)}, u32[]{:S(2)}) copy-start(bf16[1024,128]{1,0:T(8,128)(2,1)} %param.6) | copy-start | bytes 786436
  0.6 70.0 %copy-start.3 = (bf16[1024,128]{1,0:T(8,128)(2,1)S(1)}, bf16[1024,128]{1,0:T(8,128)(2,1)}, u32[]{:S(2)}) copy-start(bf16[1024,128]{1,0:T(8,128)(2,1)} %param.7) | copy-start | bytes 786436
  4.7 20.7 %all-to-all-start = ((s32[64,1,1]{2,1,0:T(1,128)}), s32[64,1,1]{2,1,0:T(1,128)S(1)}, u32[]{:S(2)}, u32[]{:S(2)}) async-start(s32[64,1,1]{2,1,0:T(1,128)} %copy.75), calls=%async_computation | async-start | bytes 65536 | tf_op jit(solution)/shard_map/all_to_all | solution.py:78
  29.8 34.4 %all-to-all-start.1 = ((bf16[64,1,64,128]{3,2,1,0:T(8,128)(2,1)}), bf16[64,1,64,128]{3,2,1,0:T(8,128)(2,1)S(1)}, u32[]{:S(2)}, u32[]{:S(2)}) async-start(bf16[64,1,64,128]{3,2,1,0:T(8,128)(2,1)} %bitcast.8), calls=%async_computation.1 | async-start | bytes 2097152 | tf_op jit(solution)/shard_map/all_to_all | solution.py:88
  36.6 34.1 %collective-permute-start = (bf16[256,256]{1,0:T(8,128)(2,1)S(1)}, bf16[256,256]{1,0:T(8,128)(2,1)S(1)}, u32[]{:S(2)}, u32[]{:S(2)}) collective-permute-start(bf16[256,256]{1,0:T(8,128)(2,1)S(1)} %get-tuple-element.25), channel_id=1, source_target_pairs={{0,1},{1,2},{2,3},{3,0},{4,5},{5,6},{6,7},{7,4},{8,9},{9,10},{10,1... | collective-permute-start | bytes 393224 | tf_op jit(solution)/shard_map/ppermute | solution.py:41
  38.1 36.1 %collective-permute-start.1 = (bf16[256,256]{1,0:T(8,128)(2,1)S(1)}, bf16[256,256]{1,0:T(8,128)(2,1)S(1)}, u32[]{:S(2)}, u32[]{:S(2)}) collective-permute-start(bf16[256,256]{1,0:T(8,128)(2,1)S(1)} %get-tuple-element.24), channel_id=1, source_target_pairs={{0,2},{1,3},{2,0},{3,1},{4,6},{5,7},{6,4},{7,5},{8,10},{9,11},{10,... | collective-permute-start | bytes 393224 | tf_op jit(solution)/shard_map/ppermute | solution.py:41
  40.9 33.3 %collective-permute-start.2 = (bf16[256,256]{1,0:T(8,128)(2,1)S(1)}, bf16[256,256]{1,0:T(8,128)(2,1)S(1)}, u32[]{:S(2)}, u32[]{:S(2)}) collective-permute-start(bf16[256,256]{1,0:T(8,128)(2,1)S(1)} %get-tuple-element.23), channel_id=1, source_target_pairs={{0,3},{1,0},{2,1},{3,2},{4,7},{5,4},{6,5},{7,6},{8,11},{9,8},{10,9... | collective-permute-start | bytes 393224 | tf_op jit(solution)/shard_map/ppermute | solution.py:41
  44.1 33.0 %collective-permute-start.6 = (bf16[256,256]{1,0:T(8,128)(2,1)}, bf16[256,256]{1,0:T(8,128)(2,1)S(1)}, u32[]{:S(2)}, u32[]{:S(2)}) collective-permute-start(bf16[256,256]{1,0:T(8,128)(2,1)} %get-tuple-element.17), channel_id=1, source_target_pairs={{0,1},{1,2},{2,3},{3,0},{4,5},{5,6},{6,7},{7,4},{8,9},{9,10},{10,1... | collective-permute-start | bytes 393224 | tf_op jit(solution)/shard_map/ppermute | solution.py:41
  44.7 32.4 %collective-permute-start.7 = (bf16[256,256]{1,0:T(8,128)(2,1)S(1)}, bf16[256,256]{1,0:T(8,128)(2,1)S(1)}, u32[]{:S(2)}, u32[]{:S(2)}) collective-permute-start(bf16[256,256]{1,0:T(8,128)(2,1)S(1)} %get-tuple-element.16), channel_id=1, source_target_pairs={{0,2},{1,3},{2,0},{3,1},{4,6},{5,7},{6,4},{7,5},{8,10},{9,11},{10,... | collective-permute-start | bytes 393224 | tf_op jit(solution)/shard_map/ppermute | solution.py:41
  65.8 21.0 %all-to-all-start.2 = ((bf16[4,14,64,128]{3,2,1,0:T(8,128)(2,1)}), bf16[4,14,64,128]{3,2,1,0:T(8,128)(2,1)S(1)}, u32[]{:S(2)}, u32[]{:S(2)}) async-start(bf16[4,14,64,128]{3,2,1,0:T(8,128)(2,1)} %bitcast.10), calls=%async_computation.2 | async-start | bytes 1835008 | tf_op jit(solution)/shard_map/all_to_all | solution.py:93
  70.7 13.6 %collective-permute-start.8 = (bf16[256,256]{1,0:T(8,128)(2,1)S(1)}, bf16[256,256]{1,0:T(8,128)(2,1)}, u32[]{:S(2)}, u32[]{:S(2)}) collective-permute-start(bf16[256,256]{1,0:T(8,128)(2,1)S(1)} %get-tuple-element.15), channel_id=1, source_target_pairs={{0,3},{1,0},{2,1},{3,2},{4,7},{5,4},{6,5},{7,6},{8,11},{9,8},{10,9... | collective-permute-start | bytes 393224 | tf_op jit(solution)/shard_map/ppermute | solution.py:41
  74.2 14.1 %copy-start.7 = (s32[1024]{0:T(1024)}, s32[1024]{0:T(1024)S(1)}, u32[]{:S(2)}) copy-start(s32[1024]{0:T(1024)S(1)} %pad_clamp_fusion.1) | copy-start | bytes 12292
  74.2 0.7 copy-start.5
  86.9 7.4 %copy-start.4 = (bf16[14,4,64,128]{3,2,1,0:T(8,128)(2,1)}, bf16[14,4,64,128]{3,2,1,0:T(8,128)(2,1)S(1)}, u32[]{:S(2)}) copy-start(bf16[14,4,64,128]{3,2,1,0:T(8,128)(2,1)S(1)} %copy.76) | copy-start | bytes 2752516
  92.1 6.4 %copy-start = (f32[2,8,1,128,128]{4,3,1,0,2:T(8,128)}, f32[2,8,1,128,128]{4,3,1,0,2:T(8,128)S(1)}, u32[]{:S(2)}) copy-start(f32[2,8,1,128,128]{4,3,1,0,2:T(8,128)S(1)} %fusion.16) | copy-start | bytes 3145732
  97.2 2.0 %copy-start.1 = (bf16[2,8,128,8,128]{2,4,1,3,0:T(8,128)(2,1)}, bf16[2,8,128,8,128]{2,4,1,3,0:T(8,128)(2,1)S(1)}, u32[]{:S(2)}) copy-start(bf16[2,8,128,8,128]{2,4,1,3,0:T(8,128)(2,1)S(1)} %fusion.1) | copy-start | bytes 12582916
  100.3 15.2 %all-to-all-start.3 = ((bf16[4,14,64,128]{3,2,1,0:T(8,128)(2,1)}), bf16[4,14,64,128]{3,2,1,0:T(8,128)(2,1)S(1)}, u32[]{:S(2)}, u32[]{:S(2)}) async-start(bf16[4,14,64,128]{3,2,1,0:T(8,128)(2,1)} %copy.92), calls=%async_computation.3 | async-start | bytes 1835008 | tf_op jit(solution)/shard_map/all_to_all | solution.py:157
  117.4 15.7 %copy-start.8 = (s32[64]{0:T(128)S(1)}, s32[64]{0:T(128)}, u32[]{:S(2)}) copy-start(s32[64]{0:T(128)} %get-tuple-element.4) | copy-start | bytes 772
  117.4 37.0 %all-to-all-start.4 = ((bf16[64,1,64,128]{3,2,1,0:T(8,128)(2,1)}), bf16[64,1,64,128]{3,2,1,0:T(8,128)(2,1)}, u32[]{:S(2)}, u32[]{:S(2)}) async-start(bf16[64,1,64,128]{3,2,1,0:T(8,128)(2,1)} %bitcast.72), calls=%async_computation.4 | async-start | bytes 2097152 | tf_op jit(solution)/shard_map/all_to_all | solution.py:167
  132.4 10.9 %collective-permute-start.9 = (bf16[256,256]{1,0:T(8,128)(2,1)S(1)}, bf16[256,256]{1,0:T(8,128)(2,1)S(1)}, u32[]{:S(2)}, u32[]{:S(2)}) collective-permute-start(bf16[256,256]{1,0:T(8,128)(2,1)S(1)} %bitcast.241), channel_id=1, source_target_pairs={{0,1},{1,2},{2,3},{3,0},{4,5},{5,6},{6,7},{7,4},{8,9},{9,10},{10,1... | collective-permute-start | bytes 393224 | tf_op jit(solution)/shard_map/ppermute | solution.py:41
  133.7 30.1 %collective-permute-start.10 = (bf16[256,256]{1,0:T(8,128)(2,1)}, bf16[256,256]{1,0:T(8,128)(2,1)}, u32[]{:S(2)}, u32[]{:S(2)}) collective-permute-start(bf16[256,256]{1,0:T(8,128)(2,1)} %bitcast.205), channel_id=1, source_target_pairs={{0,2},{1,3},{2,0},{3,1},{4,6},{5,7},{6,4},{7,5},{8,10},{9,11},{10,... | collective-permute-start | bytes 393224 | tf_op jit(solution)/shard_map/ppermute | solution.py:41
  136.5 27.4 %collective-permute-start.11 = (bf16[256,256]{1,0:T(8,128)(2,1)}, bf16[256,256]{1,0:T(8,128)(2,1)}, u32[]{:S(2)}, u32[]{:S(2)}) collective-permute-start(bf16[256,256]{1,0:T(8,128)(2,1)} %bitcast.204), channel_id=1, source_target_pairs={{0,3},{1,0},{2,1},{3,2},{4,7},{5,4},{6,5},{7,6},{8,11},{9,8},{10,9... | collective-permute-start | bytes 393224 | tf_op jit(solution)/shard_map/ppermute | solution.py:41
  138.4 28.1 %collective-permute-start.3 = (bf16[256,256]{1,0:T(8,128)(2,1)}, bf16[256,256]{1,0:T(8,128)(2,1)}, u32[]{:S(2)}, u32[]{:S(2)}) collective-permute-start(bf16[256,256]{1,0:T(8,128)(2,1)} %bitcast.210), channel_id=1, source_target_pairs={{0,1},{1,2},{2,3},{3,0},{4,5},{5,6},{6,7},{7,4},{8,9},{9,10},{10,1... | collective-permute-start | bytes 393224 | tf_op jit(solution)/shard_map/ppermute | solution.py:41
  140.5 26.0 %collective-permute-start.4 = (bf16[256,256]{1,0:T(8,128)(2,1)}, bf16[256,256]{1,0:T(8,128)(2,1)}, u32[]{:S(2)}, u32[]{:S(2)}) collective-permute-start(bf16[256,256]{1,0:T(8,128)(2,1)} %bitcast.209), channel_id=1, source_target_pairs={{0,2},{1,3},{2,0},{3,1},{4,6},{5,7},{6,4},{7,5},{8,10},{9,11},{10,... | collective-permute-start | bytes 393224 | tf_op jit(solution)/shard_map/ppermute | solution.py:41
  143.4 0.6 copy-start.6
  144.0 22.5 %collective-permute-start.5 = (bf16[256,256]{1,0:T(8,128)(2,1)}, bf16[256,256]{1,0:T(8,128)(2,1)}, u32[]{:S(2)}, u32[]{:S(2)}) collective-permute-start(bf16[256,256]{1,0:T(8,128)(2,1)} %bitcast.208), channel_id=1, source_target_pairs={{0,3},{1,0},{2,1},{3,2},{4,7},{5,4},{6,5},{7,6},{8,11},{9,8},{10,9... | collective-permute-start | bytes 393224 | tf_op jit(solution)/shard_map/ppermute | solution.py:41
  160.4 10.1 %all-to-all-start.5 = ((f32[4,2,64,128]{3,2,1,0:T(8,128)}), f32[4,2,64,128]{3,2,1,0:T(8,128)S(1)}, u32[]{:S(2)}, u32[]{:S(2)}) async-start(f32[4,2,64,128]{3,2,1,0:T(8,128)} %bitcast.75), calls=%async_computation.5 | async-start | bytes 524288 | tf_op jit(solution)/shard_map/all_to_all | solution.py:180
